TPU v7x, 32 devices: a whole 2x2x4 slice. The times are simulated.
32 devices in a mesh: dp: 16 (over z, y, x), stream: 2 (over core).
Axes of the slice: x: 2, y: 2, z: 4, core: 2. Of those that a mesh axis runs over, the one named last changes fastest.
Arguments:
- feats: float32 [256, 180, 128], P('dp', 'stream'), may hold values from -6 to 6
- occupied: int32 [256, 180], P('dp', 'stream'), may hold values from 0 to 1, as said below
- cotangent: float32 [256, 180, 70], P('dp', 'stream'), may hold values from -6 to 6
- vector_params: float32 [1734], replicated, may hold values from 0.5 to 1.5
- vector_moment: float32 [1734], replicated, may hold values from -40 to 40
- vector_square: float32 [1734], replicated, may hold values from 216.576 to 875.52
- down_weight: float32 [1152, 256], P('dp'), may hold values from -0.1875 to 0.1875
- down_moment: float32 [1152, 256], P('dp'), may hold values from -16 to 16
- down_square: float32 [1152, 256], P('dp'), may hold values from 35.0208 to 138.24
- down_gram: float32 [256, 256], replicated, as said below
- down_basis: float32 [256, 256], replicated, as said below
- upward_weight: float32 [1024, 256], P('dp'), may hold values from -0.375 to 0.375
- upward_moment: float32 [1024, 256], P('dp'), may hold values from -10 to 10
- upward_square: float32 [1024, 256], P('dp'), may hold values from 11.9808 to 46.08
- upward_gram: float32 [256, 256], replicated, as said below
- upward_basis: float32 [256, 256], replicated, as said below
- lateral_weight: float32 [128, 256], replicated, may hold values from -0.5 to 0.5
- lateral_moment: float32 [128, 256], replicated, may hold values from -20 to 20
- lateral_square: float32 [128, 256], replicated, may hold values from 55.296 to 216.576
- lateral_gram: float32 [256, 256], replicated, as said below
- lateral_basis: float32 [256, 256], replicated, as said below
- merging_weight: float32 [4608, 64], P('dp'), may hold values from -0.09375 to 0.09375
- merging_moment: float32 [4608, 64], P('dp'), may hold values from -64 to 64
- merging_square: float32 [4608, 64], P('dp'), may hold values from 599.04 to 2442.24
- merging_gram: float32 [64, 64], replicated, as said below
- merging_basis: float32 [64, 64], replicated, as said below
- heads_weight: float32 [64, 70], replicated, may hold values from -0.75 to 0.75
- heads_moment: float32 [64, 70], replicated, may hold values from -128 to 128
- heads_square: float32 [64, 70], replicated, may hold values from 2442.24 to 9676.8
- heads_gram: float32 [70, 70], replicated, as said below
- heads_basis: float32 [70, 70], replicated, as said below
Outputs:
- head_maps: float32 [256, 180, 70], P('dp', 'stream')
- feats_grad: float32 [256, 180, 128], P('dp', 'stream')
- vector_renewed: float32 [1734], replicated
- vector_momentum: float32 [1734], replicated
- vector_variance: float32 [1734], replicated
- down_renewed: float32 [1152, 256], P('dp')
- down_momentum: float32 [1152, 256], P('dp')
- down_variance: float32 [1152, 256], P('dp')
- down_gramian: float32 [256, 256], replicated
- down_rotation: float32 [256, 256], replicated
- upward_renewed: float32 [1024, 256], P('dp')
- upward_momentum: float32 [1024, 256], P('dp')
- upward_variance: float32 [1024, 256], P('dp')
- upward_gramian: float32 [256, 256], replicated
- upward_rotation: float32 [256, 256], replicated
- lateral_renewed: float32 [128, 256], replicated
- lateral_momentum: float32 [128, 256], replicated
- lateral_variance: float32 [128, 256], replicated
- lateral_gramian: float32 [256, 256], replicated
- lateral_rotation: float32 [256, 256], replicated
- merging_renewed: float32 [4608, 64], P('dp')
- merging_momentum: float32 [4608, 64], P('dp')
- merging_variance: float32 [4608, 64], P('dp')
- merging_gramian: float32 [64, 64], replicated
- merging_rotation: float32 [64, 64], replicated
- heads_renewed: float32 [64, 70], replicated
- heads_momentum: float32 [64, 70], replicated
- heads_variance: float32 [64, 70], replicated
- heads_gramian: float32 [70, 70], replicated
- heads_rotation: float32 [70, 70], replicated
Inputs may be any that keep to these rules, and one draw needn't show every extreme that they name: 1 marks an occupied pixel. `down_gram`: symmetric. `upward_gram`: symmetric. `lateral_gram`: symmetric. `merging_gram`: symmetric. `heads_gram`: symmetric. `down_basis`: orthogonal. `upward_basis`: orthogonal. `lateral_basis`: orthogonal. `merging_basis`: orthogonal. `heads_basis`: orthogonal.
All inputs are finite; a program needn't handle non-finite values.
Results may differ from a plain program's by a relative error of at most 0.0003.
Values sent between devices are 32-bit elements; how exact they have to be, the bound alone decides.
No kernel may reach another device: no remote copies, remote signals or barrier semaphores. Data moves between devices by JAX's collectives and lax.ppermute only.
A program may use at most 128 MiB of HBM per device.

v0:
```python
import math

import jax
import jax.numpy as jnp
from jax import lax
from jax.sharding import PartitionSpec as P

C0 = 128
C1 = 256
C2 = 64
CH = 70
SCENE_ROWS = 180
STEP = 10


EPS_NORM = 1e-05
BETA_ONE = 0.9
BETA_TWO = 0.95
BETA_GRAM = 0.95
EPS_ADAM = 1e-08
DECAY = 0.01
VECTOR_RATE = 0.1
HIGHEST = lax.Precision.HIGHEST


def from_behind(block, axis, distance):
    devices = range(lax.axis_size(axis))
    route = [(i - distance, i) for i in devices if i - distance in devices]
    return lax.ppermute(block, axis, route)


def shifted(value, axis, steps):
    count = lax.axis_size(axis)
    pairs = [(source, (source + steps) % count) for source in range(count)]
    return lax.ppermute(value, axis, pairs)


def extended_2(shard, sides, width):
    for axis, dim in sides:
        count, length = (lax.axis_size(axis), shard.shape[dim])
        up = [(i, (i + 1) % count) for i in range(count)]
        down = [(j, i) for i, j in up]
        last = lax.slice_in_dim(shard, length - width, length, axis=dim)
        initial = lax.slice_in_dim(shard, 0, width, axis=dim)
        before = lax.ppermute(last, axis, up)
        after = lax.ppermute(initial, axis, down)
        shard = jnp.concatenate([before, shard, after], axis=dim)
    return shard


def matmul(left, right):
    return jnp.dot(left, right, precision=HIGHEST, preferred_element_type=jnp.float32)


def contract(left, right):
    return jnp.tensordot(left, right, axes=((0, 1), (0, 1)), precision=HIGHEST)


def back_product(upstream, matrix):
    return jnp.tensordot(upstream, matrix, axes=((2,), (1,)), precision=HIGHEST)


def gram_rows(gradient):
    return jnp.tensordot(gradient, gradient, axes=((0,), (0,)), precision=HIGHEST)


def keep_rows(global_rows, total_rows):
    wrapped = jnp.remainder(global_rows, total_rows)
    return ((wrapped + SCENE_ROWS // 2) % SCENE_ROWS != 0).astype(jnp.float32)


def split_vector(packed):
    widths = [C1] * 6 + [C2] * 2 + [CH]
    pieces = []
    offset = 0
    for extent in widths:
        pieces.append(packed[offset : offset + extent])
        offset = offset + extent
    return pieces


def assemble_quads(quads):
    paired = [jnp.stack(quads[parity], axis=2) for parity in range(2)]
    joined = jnp.stack(paired, axis=1)
    return joined.reshape(joined.shape[0] * 2, joined.shape[2] * 2, joined.shape[4])


def split_quads(feature):
    shaped = feature.reshape(feature.shape[0] // 2, 2, feature.shape[1] // 2, 2, feature.shape[2])
    return [[shaped[:, row_tap, :, col_tap] for col_tap in range(2)] for row_tap in range(2)]


def norm_forward(feature, norm_gain, norm_shift, pixels):
    totals = lax.psum(
        (jnp.sum(feature, axis=(0, 1)), jnp.sum(feature * feature, axis=(0, 1))), ("dp", "stream")
    )
    centre = totals[0] / pixels
    spread = lax.rsqrt(totals[1] / pixels - centre * centre + EPS_NORM)
    normed = (feature - centre) * spread
    return (jax.nn.silu(norm_gain * normed + norm_shift), normed, spread)


def norm_backward(upstream, normed, spread, norm_gain, norm_shift, pixels):
    hidden = norm_gain * normed + norm_shift
    sigmoid = jax.nn.sigmoid(hidden)
    grad_hidden = upstream * sigmoid * (1.0 + hidden * (1.0 - sigmoid))
    grad_gain, grad_shift = lax.psum(
        (jnp.sum(grad_hidden * normed, axis=(0, 1)), jnp.sum(grad_hidden, axis=(0, 1))),
        ("dp", "stream"),
    )
    grad_feature = (
        norm_gain * spread * (grad_hidden - grad_shift / pixels - normed * (grad_gain / pixels))
    )
    return (grad_feature, grad_gain, grad_shift)


def adam_vector(params, moment, square, gradient):
    momentum = BETA_ONE * moment + (1.0 - BETA_ONE) * gradient
    variance = BETA_TWO * square + (1.0 - BETA_TWO) * gradient * gradient
    direction = (
        momentum / (1.0 - BETA_ONE**STEP) / (jnp.sqrt(variance / (1.0 - BETA_TWO**STEP)) + EPS_ADAM)
    )
    return (params - VECTOR_RATE * (direction + DECAY * params), momentum, variance)


def soap_step(weight, moment, square, gram_old, basis_old, gradient, gram_sum, step_rate):
    rotated = matmul(gradient, basis_old)
    momentum = BETA_ONE * moment + (1.0 - BETA_ONE) * rotated
    variance = BETA_TWO * square + (1.0 - BETA_TWO) * rotated * rotated
    direction = (
        momentum / (1.0 - BETA_ONE**STEP) / (jnp.sqrt(variance / (1.0 - BETA_TWO**STEP)) + EPS_ADAM)
    )
    renewed = weight - step_rate * (matmul(direction, basis_old.T) + DECAY * weight)
    gramian = BETA_GRAM * gram_old + (1.0 - BETA_GRAM) * gram_sum
    product = matmul(gramian, basis_old)
    factor = jnp.linalg.cholesky(matmul(product.T, product))
    rotation = jax.scipy.linalg.solve_triangular(factor, product.T, lower=True).T
    return (renewed, momentum, variance, gramian, rotation)


def local(
    feats,
    occupied,
    cotangent,
    vector_params,
    vector_moment,
    vector_square,
    down_weight,
    down_moment,
    down_square,
    down_gram,
    down_basis,
    upward_weight,
    upward_moment,
    upward_square,
    upward_gram,
    upward_basis,
    lateral_weight,
    lateral_moment,
    lateral_square,
    lateral_gram,
    lateral_basis,
    merging_weight,
    merging_moment,
    merging_square,
    merging_gram,
    merging_basis,
    heads_weight,
    heads_moment,
    heads_square,
    heads_gram,
    heads_basis,
):
    height, breadth, channels = feats.shape
    half_height, half_breadth = (height // 2, breadth // 2)
    total_rows = height * lax.axis_size("dp")
    fine_count = float(height * breadth * lax.axis_size("dp") * lax.axis_size("stream"))
    coarse_count = fine_count / 4.0
    first_row = lax.axis_index("dp") * height
    stream_index = lax.axis_index("stream")
    left_live = (stream_index != 0).astype(jnp.float32)
    right_live = (stream_index != lax.axis_size("stream") - 1).astype(jnp.float32)
    column_mask = jnp.concatenate(
        [left_live[None], jnp.ones((breadth,), jnp.float32), right_live[None]]
    )[None, :, None]
    down_full, upward_full, merging_full = (
        lax.all_gather(down_weight, "dp", axis=0, tiled=True),
        lax.all_gather(upward_weight, "dp", axis=0, tiled=True),
        lax.all_gather(merging_weight, "dp", axis=0, tiled=True),
    )
    (
        gain_one,
        shift_one,
        gain_three,
        shift_three,
        gain_four,
        shift_four,
        gain_five,
        shift_five,
        head_bias,
    ) = split_vector(vector_params)
    occupancy = occupied.astype(jnp.float32)[..., None]
    masked = feats * occupancy
    left_edge = from_behind(masked[:, breadth - 1 :], "stream", 1)
    widened = jnp.concatenate([left_edge, masked], axis=1)
    upper_edge = shifted(widened[height - 1 :], "dp", 1)
    padded = jnp.concatenate([upper_edge, widened], axis=0)
    coarse_keep = keep_rows(first_row + 2 * jnp.arange(half_height), total_rows)[:, None, None]
    windows = [
        [
            padded[row_tap : row_tap + height : 2, col_tap : col_tap + breadth : 2]
            for col_tap in range(3)
        ]
        for row_tap in range(3)
    ]
    coarse = jnp.zeros((half_height, half_breadth, C1), jnp.float32)
    for row_tap in range(3):
        for col_tap in range(3):
            offset = (3 * row_tap + col_tap) * channels
            contrib = matmul(windows[row_tap][col_tap], down_full[offset : offset + channels])
            if row_tap == 0:
                contrib = contrib * coarse_keep
            coarse = coarse + contrib
    act_one, normed_one, spread_one = norm_forward(coarse, gain_one, shift_one, coarse_count)
    quads = [
        [
            matmul(
                act_one,
                upward_full[(2 * row_tap + col_tap) * C1 : (2 * row_tap + col_tap + 1) * C1],
            )
            for col_tap in range(2)
        ]
        for row_tap in range(2)
    ]
    act_three, normed_three, spread_three = norm_forward(
        assemble_quads(quads), gain_three, shift_three, fine_count
    )
    act_four, normed_four, spread_four = norm_forward(
        matmul(masked, lateral_weight), gain_four, shift_four, fine_count
    )
    joined = jnp.concatenate([act_three, act_four], axis=2)
    framed = extended_2(joined, (("dp", 0), ("stream", 1)), 1) * column_mask
    row_index = first_row + jnp.arange(height)
    row_keeps = [
        keep_rows(row_index, total_rows)[:, None, None],
        None,
        keep_rows(row_index + 1, total_rows)[:, None, None],
    ]
    merged = jnp.zeros((height, breadth, C2), jnp.float32)
    for row_tap in range(3):
        for col_tap in range(3):
            offset = (3 * row_tap + col_tap) * 2 * C1
            contrib = matmul(
                framed[row_tap : row_tap + height, col_tap : col_tap + breadth],
                merging_full[offset : offset + 2 * C1],
            )
            if row_tap != 1:
                contrib = contrib * row_keeps[row_tap]
            merged = merged + contrib
    act_five, normed_five, spread_five = norm_forward(merged, gain_five, shift_five, fine_count)
    head_maps = matmul(act_five, heads_weight) + head_bias
    grad_heads = contract(act_five, cotangent)
    grad_bias = jnp.sum(cotangent, axis=(0, 1))
    grad_five = back_product(cotangent, heads_weight)
    grad_merged, gain_grad_five, shift_grad_five = norm_backward(
        grad_five, normed_five, spread_five, gain_five, shift_five, fine_count
    )
    grad_framed = extended_2(grad_merged, (("dp", 0), ("stream", 1)), 1) * column_mask
    frame_rows = first_row - 1 + jnp.arange(height + 2)
    frame_keeps = [
        keep_rows(frame_rows, total_rows)[:, None, None],
        None,
        keep_rows(frame_rows + 1, total_rows)[:, None, None],
    ]
    merging_parts = []
    grad_joined = jnp.zeros((height, breadth, 2 * C1), jnp.float32)
    for row_tap in range(3):
        if row_tap == 1:
            local_grad = grad_merged
            source_frame = grad_framed
        else:
            local_grad = grad_merged * row_keeps[row_tap]
            source_frame = grad_framed * frame_keeps[row_tap]
        for col_tap in range(3):
            offset = (3 * row_tap + col_tap) * 2 * C1
            merging_parts.append(
                contract(
                    framed[row_tap : row_tap + height, col_tap : col_tap + breadth], local_grad
                )
            )
            grad_joined = grad_joined + back_product(
                source_frame[
                    2 - row_tap : 2 - row_tap + height, 2 - col_tap : 2 - col_tap + breadth
                ],
                merging_full[offset : offset + 2 * C1],
            )
    grad_merging = jnp.concatenate(merging_parts, axis=0)
    grad_lateral_map, gain_grad_four, shift_grad_four = norm_backward(
        grad_joined[:, :, C1:], normed_four, spread_four, gain_four, shift_four, fine_count
    )
    grad_lateral = contract(masked, grad_lateral_map)
    grad_masked = back_product(grad_lateral_map, lateral_weight)
    grad_upsampled, gain_grad_three, shift_grad_three = norm_backward(
        grad_joined[:, :, :C1], normed_three, spread_three, gain_three, shift_three, fine_count
    )
    up_quads = split_quads(grad_upsampled)
    upward_parts = []
    grad_act_one = jnp.zeros((half_height, half_breadth, C1), jnp.float32)
    for row_tap in range(2):
        for col_tap in range(2):
            offset = (2 * row_tap + col_tap) * C1
            upward_parts.append(contract(act_one, up_quads[row_tap][col_tap]))
            grad_act_one = grad_act_one + back_product(
                up_quads[row_tap][col_tap], upward_full[offset : offset + C1]
            )
    grad_upward = jnp.concatenate(upward_parts, axis=0)
    grad_coarse, gain_grad_one, shift_grad_one = norm_backward(
        grad_act_one, normed_one, spread_one, gain_one, shift_one, coarse_count
    )
    down_parts = []
    for row_tap in range(3):
        local_grad = grad_coarse * coarse_keep if row_tap == 0 else grad_coarse
        for col_tap in range(3):
            down_parts.append(contract(windows[row_tap][col_tap], local_grad))
    grad_down = jnp.concatenate(down_parts, axis=0)
    right_edge = from_behind(grad_coarse[:, :1], "stream", -1)
    extended = jnp.concatenate([grad_coarse, right_edge], axis=1)
    lower_edge = shifted(extended[:1], "dp", -1)
    extended = jnp.concatenate([extended, lower_edge], axis=0)
    extended_keep = keep_rows(first_row + 2 * jnp.arange(half_height + 1), total_rows)[
        :, None, None
    ]
    parity_taps = [[1], [0, 2]]
    back_quads = []
    for row_parity in range(2):
        quad_row = []
        for col_parity in range(2):
            total_piece = jnp.zeros((half_height, half_breadth, channels), jnp.float32)
            for row_tap in parity_taps[row_parity]:
                for col_tap in parity_taps[col_parity]:
                    row_start = 1 if row_tap == 0 else 0
                    col_start = 1 if col_tap == 0 else 0
                    source = extended[
                        row_start : row_start + half_height, col_start : col_start + half_breadth
                    ]
                    if row_tap == 0:
                        source = source * extended_keep[1 : half_height + 1]
                    tap_offset = (3 * row_tap + col_tap) * channels
                    total_piece = total_piece + back_product(
                        source, down_full[tap_offset : tap_offset + channels]
                    )
            quad_row.append(total_piece)
        back_quads.append(quad_row)
    grad_masked = grad_masked + assemble_quads(back_quads)
    feats_grad = grad_masked * occupancy
    dp_index = lax.axis_index("dp")
    total_down, total_upward, total_lateral, total_merging, total_heads, total_bias = lax.psum(
        (grad_down, grad_upward, grad_lateral, grad_merging, grad_heads, grad_bias),
        ("dp", "stream"),
    )
    down_shard = lax.dynamic_slice_in_dim(
        total_down, dp_index * down_weight.shape[0], down_weight.shape[0], 0
    )
    upward_shard = lax.dynamic_slice_in_dim(
        total_upward, dp_index * upward_weight.shape[0], upward_weight.shape[0], 0
    )
    merging_shard = lax.dynamic_slice_in_dim(
        total_merging, dp_index * merging_weight.shape[0], merging_weight.shape[0], 0
    )
    gram_down = gram_rows(total_down)
    gram_upward = gram_rows(total_upward)
    gram_merging = gram_rows(total_merging)
    grad_vector = jnp.concatenate(
        [
            gain_grad_one,
            shift_grad_one,
            gain_grad_three,
            shift_grad_three,
            gain_grad_four,
            shift_grad_four,
            gain_grad_five,
            shift_grad_five,
            total_bias,
        ]
    )
    vector_renewed, vector_momentum, vector_variance = adam_vector(
        vector_params, vector_moment, vector_square, grad_vector
    )
    down_renewed, down_momentum, down_variance, down_gramian, down_rotation = soap_step(
        down_weight,
        down_moment,
        down_square,
        down_gram,
        down_basis,
        down_shard,
        gram_down,
        1.0 / math.sqrt(9 * C0),
    )
    upward_renewed, upward_momentum, upward_variance, upward_gramian, upward_rotation = soap_step(
        upward_weight,
        upward_moment,
        upward_square,
        upward_gram,
        upward_basis,
        upward_shard,
        gram_upward,
        1.0 / math.sqrt(C1),
    )
    lateral_renewed, lateral_momentum, lateral_variance, lateral_gramian, lateral_rotation = (
        soap_step(
            lateral_weight,
            lateral_moment,
            lateral_square,
            lateral_gram,
            lateral_basis,
            total_lateral,
            gram_rows(total_lateral),
            1.0 / math.sqrt(C0),
        )
    )
    merging_renewed, merging_momentum, merging_variance, merging_gramian, merging_rotation = (
        soap_step(
            merging_weight,
            merging_moment,
            merging_square,
            merging_gram,
            merging_basis,
            merging_shard,
            gram_merging,
            1.0 / math.sqrt(18 * C1),
        )
    )
    heads_renewed, heads_momentum, heads_variance, heads_gramian, heads_rotation = soap_step(
        heads_weight,
        heads_moment,
        heads_square,
        heads_gram,
        heads_basis,
        total_heads,
        gram_rows(total_heads),
        1.0 / math.sqrt(C2),
    )
    return (
        head_maps,
        feats_grad,
        vector_renewed,
        vector_momentum,
        vector_variance,
        down_renewed,
        down_momentum,
        down_variance,
        down_gramian,
        down_rotation,
        upward_renewed,
        upward_momentum,
        upward_variance,
        upward_gramian,
        upward_rotation,
        lateral_renewed,
        lateral_momentum,
        lateral_variance,
        lateral_gramian,
        lateral_rotation,
        merging_renewed,
        merging_momentum,
        merging_variance,
        merging_gramian,
        merging_rotation,
        heads_renewed,
        heads_momentum,
        heads_variance,
        heads_gramian,
        heads_rotation,
    )


def solution(mesh):
    in_specs = (
        P("dp", "stream", None),
        P("dp", "stream"),
        P("dp", "stream", None),
        P(),
        P(),
        P(),
        P("dp", None),
        P("dp", None),
        P("dp", None),
        P(),
        P(),
        P("dp", None),
        P("dp", None),
        P("dp", None),
        P(),
        P(),
        P(),
        P(),
        P(),
        P(),
        P(),
        P("dp", None),
        P("dp", None),
        P("dp", None),
        P(),
        P(),
        P(),
        P(),
        P(),
        P(),
        P(),
    )
    out_specs = (
        P("dp", "stream", None),
        P("dp", "stream", None),
        P(),
        P(),
        P(),
        P("dp", None),
        P("dp", None),
        P("dp", None),
        P(),
        P(),
        P("dp", None),
        P("dp", None),
        P("dp", None),
        P(),
        P(),
        P(),
        P(),
        P(),
        P(),
        P(),
        P("dp", None),
        P("dp", None),
        P("dp", None),
        P(),
        P(),
        P(),
        P(),
        P(),
        P(),
        P(),
    )
    return jax.shard_map(local, mesh=mesh, in_specs=in_specs, out_specs=out_specs, check_vma=False)
```

profile of v0, /device:TPU:0, one launch (start us, length us, event | category | flops | bytes accessed | tf_op | source)
XLA Modules:
  0.0 957.7 jit_solution(1342322445474177669)
XLA Ops:
  38.5 31.4 %all-gather.5.cloned.1.call-done = f32[1152,256]{1,0:T(8,128)} async-done(((f32[72,256]{1,0:T(8,128)}), f32[1152,256]{1,0:T(8,128)}) %all-gather.5.cloned.1.call-update) | async-done | bytes 1179664 | tf_op jit(solution)/shard_map/all_gather | solution.py:187
  77.2 38.8 %all-reduce.6 = (f32[256]{0:T(256)S(1)}, f32[256]{0:T(256)S(1)}) all-reduce(f32[256]{0:T(256)S(1)} %get-tuple-element.158, f32[256]{0:T(256)S(1)} %get-tuple-element.157), channel_id=1, replica_groups=mesh['dp'=16,'stream'=2] {'dp','stream'}, use_global_device_ids=true, to_apply=%region_3.4 | all-reduce | flops 512 | bytes 4096 | tf_op jit(solution)/shard_map/psum | solution.py:94
  116.0 10.8 %all-gather.7.cloned.1.call-done = f32[1024,256]{1,0:T(8,128)} async-done(((f32[64,256]{1,0:T(8,128)}), f32[1024,256]{1,0:T(8,128)}) %all-gather.7.cloned.1.call-update) | async-done | bytes 1048592 | tf_op jit(solution)/shard_map/all_gather | solution.py:188
  135.3 38.7 %all-reduce.5 = (f32[256]{0:T(256)S(1)}, f32[256]{0:T(256)S(1)}, f32[256]{0:T(256)S(1)}, f32[256]{0:T(256)S(1)}) all-reduce(f32[256]{0:T(256)S(1)} %get-tuple-element.150, f32[256]{0:T(256)S(1)} %get-tuple-element.149, f32[256]{0:T(256)S(1)} %get-tuple-element.226, ...), channel_id=1, replica_groups=mesh['dp'=16,'stream'=2] {'dp','stream'}, use_global_device_ids=true, to_apply=%region_14.15 | all-reduce | flops 1024 | bytes 8192 | tf_op jit(solution)/shard_map/psum | solution.py:94
  178.2 3.2 collective-permute-start.3
  182.1 6.6 collective-permute-done.2
  191.7 3.5 copy.106
  195.2 3.5 reshape.286
  201.0 3.8 fusion.53
  204.8 3.8 fusion.50
  208.6 3.7 fusion.47
  212.3 3.8 fusion.14
  216.1 4.0 fusion.18
  220.0 3.7 fusion.22
  223.7 3.8 fusion.26
  227.5 3.8 fusion.30
  231.4 4.3 fusion.368
  235.7 39.8 %all-reduce.4 = (f32[64]{0:T(128)S(1)}, f32[64]{0:T(128)S(1)}) all-reduce(f32[64]{0:T(128)S(1)} %get-tuple-element.154, f32[64]{0:T(128)S(1)} %get-tuple-element.153), channel_id=1, replica_groups=mesh['dp'=16,'stream'=2] {'dp','stream'}, use_global_device_ids=true, to_apply=%region_18.19 | all-reduce | flops 128 | bytes 1024 | tf_op jit(solution)/shard_map/psum | solution.py:94
  277.5 39.0 %all-reduce.3 = (f32[64]{0:T(128)S(1)}, f32[64]{0:T(128)S(1)}) all-reduce(f32[64]{0:T(128)S(1)} %get-tuple-element.152, f32[64]{0:T(128)S(1)} %get-tuple-element.151), channel_id=1, replica_groups=mesh['dp'=16,'stream'=2] {'dp','stream'}, use_global_device_ids=true, to_apply=%region_22.23 | all-reduce | flops 128 | bytes 1024 | tf_op jit(solution)/shard_map/psum | solution.py:107
  318.4 4.5 fusion.105
  325.3 3.3 collective-permute-start.7
  328.6 2.7 fusion.111
  331.3 2.7 fusion.117
  344.2 2.7 fusion.147
  346.9 2.7 fusion.153
  354.5 2.8 convolution_bitcast_fusion.15
  360.9 3.4 fusion.169
  364.3 3.2 fusion.171
  370.2 3.2 fusion.181
  373.4 3.2 fusion.183
  376.6 3.1 fusion.173
  379.7 4.9 fusion.175
  384.6 4.9 fusion.177
  389.5 5.7 add_add_fusion
  395.3 3.5 fusion.364
  398.8 37.6 %all-reduce.2 = (f32[256]{0:T(256)S(1)}, f32[256]{0:T(256)S(1)}) all-reduce(f32[256]{0:T(256)S(1)} %get-tuple-element.220, f32[256]{0:T(256)S(1)} %get-tuple-element.221), channel_id=1, replica_groups=mesh['dp'=16,'stream'=2] {'dp','stream'}, use_global_device_ids=true, to_apply=%region_30.31 | all-reduce | flops 512 | bytes 4096 | tf_op jit(solution)/shard_map/psum | solution.py:107
  436.4 2.9 subtract_multiply_fusion
  451.6 40.9 %all-reduce.1 = (f32[256]{0:T(256)S(1)}, f32[256]{0:T(256)S(1)}, f32[256]{0:T(256)}, f32[256]{0:T(256)}, f32[70]{0:T(128)}, /*index=5*/f32[64,70]{1,0:T(8,128)S(1)}) all-reduce(f32[256]{0:T(256)S(1)} %get-tuple-element.156, f32[256]{0:T(256)S(1)} %get-tuple-element.155, ...), channel_id=1, replica_groups=mesh['dp'=16,'stream'=2] {'dp','stream'}, use_global_device_ids=true, to_apply=%region_34.35 | all-reduce | flops 5574 | bytes 44592 | tf_op jit(solution)/shard_map/psum | solution.py:107
  503.5 7.8 cholesky.125
  514.8 6.8 custom-call.26
  543.3 5.0 collective-permute-start.11
  558.0 123.7 %all-reduce.10.cloned.1.call-done = (f32[1152,256]{1,0:T(8,128)}, f32[1024,256]{1,0:T(8,128)}, f32[128,256]{1,0:T(8,128)}, f32[4608,64]{0,1:T(8,128)}) async-done(((f32[1152,256]{1,0:T(8,128)}, f32[1024,256]{1,0:T(8,128)}, f32[128,256]{1,0:T(8,128)}, f32[4608,64]{0,1:T(8,128)}), (f32[1152,256]{1,0:T(8,128)}, f32[1024,256]{1,0:T(8,128)}, f32[128,256]{1,0:T(8,128)}, ...) | async-done | bytes 3538960 | tf_op jit(solution)/shard_map/psum | solution.py:357
  681.7 2.8 fusion.165
  685.1 5.8 cholesky.111
  692.2 4.9 custom-call.25
  712.5 13.2 %cholesky.310 = f32[128,128]{1,0:T(8,128)} custom-call(f32[128,128]{1,0:T(8,128)} %cholesky.346), custom_call_target="Cholesky" | custom-call | tf_op jit(solution)/shard_map/jit(cholesky)/cholesky | solution.py:136
  727.8 11.3 %custom-call.35 = f32[1,128,128]{1,2,0:T(8,128)} custom-call(f32[1,128,128]{2,1,0:T(8,128)} %get-tuple-element.244), custom_call_target="InvertDiagBlocksLowerTriangular" | custom-call | tf_op jit(solution)/shard_map/jit(cholesky)/cholesky | solution.py:136
  744.1 13.6 %cholesky.327 = f32[128,128]{1,0:T(8,128)} custom-call(f32[128,128]{1,0:T(8,128)} %convolution_subtract_fusion.3), custom_call_target="Cholesky" | custom-call | tf_op jit(solution)/shard_map/jit(cholesky)/cholesky | solution.py:136
  763.5 7.0 while.8
  764.1 2.9 bitcast_dynamic-update-slice_fusion.8
  767.6 2.9 bitcast_dynamic-update-slice_fusion.8
  770.5 21.1 %custom-call.36 = f32[2,128,128]{1,2,0:T(8,128)} custom-call(f32[2,128,128]{2,1,0:T(8,128)} %get-tuple-element.54), custom_call_target="InvertDiagBlocksLowerTriangular" | custom-call | tf_op jit(solution)/shard_map/jit(_solve_triangular)/triangular_solve | solution.py:137
  798.8 11.7 %cholesky.276 = f32[128,128]{1,0:T(8,128)S(1)} custom-call(f32[128,128]{1,0:T(8,128)S(1)} %cholesky.343), custom_call_target="Cholesky" | custom-call | tf_op jit(solution)/shard_map/jit(cholesky)/cholesky | solution.py:136
  811.2 10.4 %custom-call.33 = f32[1,128,128]{1,2,0:T(8,128)} custom-call(f32[1,128,128]{2,1,0:T(8,128)S(1)} %get-tuple-element.248), custom_call_target="InvertDiagBlocksLowerTriangular" | custom-call | tf_op jit(solution)/shard_map/jit(cholesky)/cholesky | solution.py:136
  825.3 13.2 %cholesky.293 = f32[128,128]{1,0:T(8,128)} custom-call(f32[128,128]{1,0:T(8,128)} %convolution_subtract_fusion.4), custom_call_target="Cholesky" | custom-call | tf_op jit(solution)/shard_map/jit(cholesky)/cholesky | solution.py:136
  842.7 7.0 while.7
  843.3 2.9 bitcast_dynamic-update-slice_fusion.7
  846.8 2.9 bitcast_dynamic-update-slice_fusion.7
  849.7 21.3 %custom-call.34 = f32[2,128,128]{1,2,0:T(8,128)} custom-call(f32[2,128,128]{2,1,0:T(8,128)} %get-tuple-element.53), custom_call_target="InvertDiagBlocksLowerTriangular" | custom-call | tf_op jit(solution)/shard_map/jit(_solve_triangular)/triangular_solve | solution.py:137
  876.3 11.7 %cholesky.242 = f32[128,128]{1,0:T(8,128)S(1)} custom-call(f32[128,128]{1,0:T(8,128)S(1)} %cholesky.340), custom_call_target="Cholesky" | custom-call | tf_op jit(solution)/shard_map/jit(cholesky)/cholesky | solution.py:136
  888.7 9.8 %custom-call.31 = f32[1,128,128]{1,2,0:T(8,128)S(1)} custom-call(f32[1,128,128]{2,1,0:T(8,128)S(1)} %get-tuple-element.254), custom_call_target="InvertDiagBlocksLowerTriangular" | custom-call | tf_op jit(solution)/shard_map/jit(cholesky)/cholesky | solution.py:136
  900.7 11.7 %cholesky.259 = f32[128,128]{1,0:T(8,128)S(1)} custom-call(f32[128,128]{1,0:T(8,128)S(1)} %convolution_subtract_fusion.5), custom_call_target="Cholesky" | custom-call | tf_op jit(solution)/shard_map/jit(cholesky)/cholesky | solution.py:136
  914.4 4.0 while.6
  918.4 20.5 %custom-call.32 = f32[2,128,128]{1,2,0:T(8,128)} custom-call(f32[2,128,128]{2,1,0:T(8,128)S(1)} %get-tuple-element.52), custom_call_target="InvertDiagBlocksLowerTriangular" | custom-call | tf_op jit(solution)/shard_map/jit(_solve_triangular)/triangular_solve | solution.py:137
  (563 shorter events, 211.7 us)
Async XLA Ops:
  7.2 699.4 %copy-start = (f32[256,256]{1,0:T(8,128)S(1)}, f32[256,256]{1,0:T(8,128)}, u32[]{:S(2)}) copy-start(f32[256,256]{1,0:T(8,128)} %param.54) | copy-start | bytes 786436
  7.2 8.9 copy-start.12
  7.2 8.3 copy-start.94
  7.2 8.9 copy-start.46
  7.3 62.6 %all-gather.5.cloned.1.call-start = ((), (), s32[]{:S(2)}) async-start(), calls=%async_computation | async-start | bytes 1253376 | tf_op jit(solution)/shard_map/all_gather | solution.py:187
  8.0 118.8 %all-gather.7.cloned.1.call-start = ((), (), s32[]{:S(2)}) async-start(), calls=%async_computation.1 | async-start | bytes 1114112 | tf_op jit(solution)/shard_map/all_gather | solution.py:188
  8.7 183.0 %all-gather.9.cloned.1.call-start = ((), (), s32[]{:S(2)}) async-start(), calls=%async_computation.2 | async-start | bytes 1671168 | tf_op jit(solution)/shard_map/all_gather | solution.py:189
  10.9 17.3 %collective-permute-start = (f32[16,1,128]{2,1,0:T(1,128)S(1)}, f32[16,1,128]{2,1,0:T(1,128)S(1)}, u32[]{:S(2)}, u32[]{:S(2)}) collective-permute-start(f32[16,1,128]{2,1,0:T(1,128)S(1)} %slice.432), channel_id=1, source_target_pairs={{0,1},{2,3},{4,5},{6,7},{8,9},{10,11},{12,13},{14,15},{16,17},{18,... | collective-permute-start | bytes 24584 | tf_op jit(solution)/shard_map/ppermute | solution.py:29
  13.3 668.4 %all-reduce.10.cloned.1.call-start = ((), (), s32[]{:S(2)}) async-start(), calls=%async_computation.3 | async-start | bytes 7077888 | tf_op jit(solution)/shard_map/psum | solution.py:357
  13.4 61.3 %copy-start.119 = (f32[8]{0:T(128)}, f32[8]{0:T(128)S(1)}, u32[]{:S(2)}) copy-start(f32[8]{0:T(128)S(1)} %compare_convert_fusion.4) | copy-start | bytes 100
  16.1 113.5 %copy-start.141 = (f32[256]{0:T(256)}, f32[256]{0:T(256)S(1)}, u32[]{:S(2)}) copy-start(f32[256]{0:T(256)S(1)} %get-tuple-element.267) | copy-start | bytes 3076
  28.2 8.6 collective-permute-start.1
  37.7 33.7 %copy-start.24 = (f32[8,45,128]{2,1,0:T(8,128)S(1)}, f32[8,45,128]{2,1,0:T(8,128)}, u32[]{:S(2)}) copy-start(f32[8,45,128]{2,1,0:T(8,128)} %slice.355) | copy-start | bytes 552964
  38.0 36.7 %copy-start.27 = (f32[8,45,128]{2,1,0:T(8,128)}, f32[8,45,128]{2,1,0:T(8,128)S(1)}, u32[]{:S(2)}) copy-start(f32[8,45,128]{2,1,0:T(8,128)S(1)} %slice.345) | copy-start | bytes 552964
  38.2 36.5 %copy-start.29 = (f32[8,45,128]{2,1,0:T(8,128)}, f32[8,45,128]{2,1,0:T(8,128)S(1)}, u32[]{:S(2)}) copy-start(f32[8,45,128]{2,1,0:T(8,128)S(1)} %slice.343) | copy-start | bytes 552964
  38.4 36.8 %copy-start.39 = (f32[8,45,128]{2,1,0:T(8,128)}, f32[8,45,128]{2,1,0:T(8,128)S(1)}, u32[]{:S(2)}) copy-start(f32[8,45,128]{2,1,0:T(8,128)S(1)} %slice.341) | copy-start | bytes 552964
  76.2 50.6 %copy-start.143 = (f32[256]{0:T(256)S(1)}, f32[256]{0:T(256)}, u32[]{:S(2)}) copy-start(f32[256]{0:T(256)} %get-tuple-element.268) | copy-start | bytes 3076
  77.2 52.5 %copy-start.41 = (f32[8,45,256]{2,1,0:T(8,128)}, f32[8,45,256]{2,1,0:T(8,128)S(1)}, u32[]{:S(2)}) copy-start(f32[8,45,256]{2,1,0:T(8,128)S(1)} %get-tuple-element.278) | copy-start | bytes 1105924
  116.0 13.7 %copy-start.134 = (f32[256]{0:T(256)}, f32[256]{0:T(256)S(1)}, u32[]{:S(2)}) copy-start(f32[256]{0:T(256)S(1)} %get-tuple-element.274) | copy-start | bytes 3076
  116.0 13.7 %copy-start.136 = (f32[256]{0:T(256)}, f32[256]{0:T(256)S(1)}, u32[]{:S(2)}) copy-start(f32[256]{0:T(256)S(1)} %get-tuple-element.275) | copy-start | bytes 3076
  135.2 39.9 %copy-start.3 = (f32[16,90,256]{2,1,0:T(8,128)}, f32[16,90,256]{2,1,0:T(8,128)S(1)}, u32[]{:S(2)}) copy-start(f32[16,90,256]{2,1,0:T(8,128)S(1)} %reshape.335) | copy-start | bytes 4423684
  174.6 220.5 %copy-start.98 = (f32[256]{0:T(256)}, f32[256]{0:T(256)S(1)}, u32[]{:S(2)}) copy-start(f32[256]{0:T(256)S(1)} %get-tuple-element.272) | copy-start | bytes 3076
  175.2 13.6 %copy-start.5 = (f32[16,90,256]{2,1,0:T(8,128)}, f32[16,90,256]{2,1,0:T(8,128)S(1)}, u32[]{:S(2)}) copy-start(f32[16,90,256]{2,1,0:T(8,128)S(1)} %fusion.38) | copy-start | bytes 4423684
  175.7 13.1 %copy-start.7 = (f32[16,90,256]{2,1,0:T(8,128)}, f32[16,90,256]{2,1,0:T(8,128)S(1)}, u32[]{:S(2)}) copy-start(f32[16,90,256]{2,1,0:T(8,128)S(1)} %fusion.39) | copy-start | bytes 4423684
  175.8 13.0 %collective-permute-start.2 = (f32[1,90,512]{2,1,0:T(8,128)S(1)}, f32[1,90,512]{2,1,0:T(8,128)S(1)}, u32[]{:S(2)}, u32[]{:S(2)}) collective-permute-start(f32[1,90,512]{2,1,0:T(8,128)S(1)} %get-tuple-element.223), channel_id=1, source_target_pairs={{0,2},{2,4},{4,6},{6,8},{8,10},{10,12},{12,14},{14,16},{16,18},{18... | collective-permute-start | bytes 552968 | tf_op jit(solution)/shard_map/ppermute | solution.py:45
  178.2 10.5 %collective-permute-start.3 = (f32[1,90,512]{2,1,0:T(8,128)S(1)}, f32[1,90,512]{2,1,0:T(8,128)S(1)}, u32[]{:S(2)}, u32[]{:S(2)}) collective-permute-start(f32[1,90,512]{2,1,0:T(8,128)S(1)} %get-tuple-element.224), channel_id=1, source_target_pairs={{2,0},{4,2},{6,4},{8,6},{10,8},{12,10},{14,12},{16,14},{18,16},{20... | collective-permute-start | bytes 552968 | tf_op jit(solution)/shard_map/ppermute | solution.py:46
  182.1 8.5 copy-start.59
  189.5 9.2 collective-permute-start.4
  189.5 9.2 collective-permute-start.5
  190.1 8.6 copy-start.124
  201.0 30.4 %copy-start.1 = (f32[18,92,512]{2,1,0:T(8,128)}, f32[18,92,512]{2,1,0:T(8,128)S(1)}, u32[]{:S(2)}) copy-start(f32[18,92,512]{2,1,0:T(8,128)S(1)} %maximum_multiply_fusion) | copy-start | bytes 10174468
  231.3 44.2 %copy-start.60 = (f32[16,90,70]{1,0,2:T(8,128)S(1)}, f32[16,90,70]{1,0,2:T(8,128)}, u32[]{:S(2)}) copy-start(f32[16,90,70]{1,0,2:T(8,128)} %param.36) | copy-start | bytes 1209604
  231.4 44.2 %copy-start.150 = (f32[64,70]{1,0:T(8,128)S(1)}, f32[64,70]{1,0:T(8,128)}, u32[]{:S(2)}) copy-start(f32[64,70]{1,0:T(8,128)} %param.60) | copy-start | bytes 53764
  235.7 113.9 %copy-start.23 = (f32[16,90,64]{1,2,0:T(8,128)}, f32[16,90,64]{1,2,0:T(8,128)S(1)}, u32[]{:S(2)}) copy-start(f32[16,90,64]{1,2,0:T(8,128)S(1)} %get-tuple-element.287) | copy-start | bytes 1105924
  275.6 74.0 %copy-start.139 = (f32[64]{0:T(128)}, f32[64]{0:T(128)S(1)}, u32[]{:S(2)}) copy-start(f32[64]{0:T(128)S(1)} %get-tuple-element.273) | copy-start | bytes 772
  275.6 74.0 %copy-start.140 = (f32[64]{0:T(128)}, f32[64]{0:T(128)S(1)}, u32[]{:S(2)}) copy-start(f32[64]{0:T(128)S(1)} %get-tuple-element.276) | copy-start | bytes 772
  275.6 74.0 %copy-start.148 = (f32[64]{0:T(128)}, f32[64]{0:T(128)S(1)}, u32[]{:S(2)}) copy-start(f32[64]{0:T(128)S(1)} %get-tuple-element.265) | copy-start | bytes 772
  275.6 74.0 %copy-start.149 = (f32[64]{0:T(128)}, f32[64]{0:T(128)S(1)}, u32[]{:S(2)}) copy-start(f32[64]{0:T(128)S(1)} %get-tuple-element.266) | copy-start | bytes 772
  318.4 10.2 %copy-start.2 = (f32[18,92,512]{2,1,0:T(8,128)S(1)}, f32[18,92,512]{2,1,0:T(8,128)}, u32[]{:S(2)}) copy-start(f32[18,92,512]{2,1,0:T(8,128)} %copy-done.1) | copy-start | bytes 10174468
  322.9 28.4 %collective-permute-start.6 = (f32[1,90,64]{1,2,0:T(8,128)S(1)}, f32[1,90,64]{1,2,0:T(8,128)S(1)}, u32[]{:S(2)}, u32[]{:S(2)}) collective-permute-start(f32[1,90,64]{1,2,0:T(8,128)S(1)} %get-tuple-element.233), channel_id=1, source_target_pairs={{0,2},{2,4},{4,6},{6,8},{8,10},{10,12},{12,14},{14,16},{16,18},{18... | collective-permute-start | bytes 69128 | tf_op jit(solution)/shard_map/ppermute | solution.py:45
  325.3 26.1 %collective-permute-start.7 = (f32[1,90,64]{1,2,0:T(8,128)S(1)}, f32[1,90,64]{1,2,0:T(8,128)S(1)}, u32[]{:S(2)}, u32[]{:S(2)}) collective-permute-start(f32[1,90,64]{1,2,0:T(8,128)S(1)} %get-tuple-element.234), channel_id=1, source_target_pairs={{2,0},{4,2},{6,4},{8,6},{10,8},{12,10},{14,12},{16,14},{18,16},{20... | collective-permute-start | bytes 69128 | tf_op jit(solution)/shard_map/ppermute | solution.py:46
  353.9 4.5 collective-permute-start.9
  354.0 4.2 collective-permute-start.8
  395.3 41.1 %copy-start.125 = (f32[256]{0:T(256)S(1)}, f32[256]{0:T(256)}, u32[]{:S(2)}) copy-start(f32[256]{0:T(256)} %get-tuple-element.258) | copy-start | bytes 3076
  450.1 42.9 %copy-start.43 = (f32[8,45,256]{2,1,0:T(8,128)S(1)}, f32[8,45,256]{2,1,0:T(8,128)}, u32[]{:S(2)}) copy-start(f32[8,45,256]{2,1,0:T(8,128)} %copy-done.41) | copy-start | bytes 1105924
  450.1 44.7 %copy-start.40 = (f32[8,45,128]{2,1,0:T(8,128)S(1)}, f32[8,45,128]{2,1,0:T(8,128)}, u32[]{:S(2)}) copy-start(f32[8,45,128]{2,1,0:T(8,128)} %copy-done.39) | copy-start | bytes 552964
  451.5 49.1 %copy-start.88 = (f32[70,70]{1,0:T(8,128)S(1)}, f32[70,70]{1,0:T(8,128)}, u32[]{:S(2)}) copy-start(f32[70,70]{1,0:T(8,128)} %param.63) | copy-start | bytes 58804
  451.5 71.7 %copy-start.30 = (f32[8,45,128]{2,1,0:T(8,128)S(1)}, f32[8,45,128]{2,1,0:T(8,128)}, u32[]{:S(2)}) copy-start(f32[8,45,128]{2,1,0:T(8,128)} %copy-done.29) | copy-start | bytes 552964
  493.0 31.9 %copy-start.28 = (f32[8,45,128]{2,1,0:T(8,128)S(1)}, f32[8,45,128]{2,1,0:T(8,128)}, u32[]{:S(2)}) copy-start(f32[8,45,128]{2,1,0:T(8,128)} %copy-done.27) | copy-start | bytes 552964
  494.2 32.6 %copy-start.38 = (f32[8,45,128]{2,1,0:T(8,128)S(1)}, f32[8,45,128]{2,1,0:T(8,128)}, u32[]{:S(2)}) copy-start(f32[8,45,128]{2,1,0:T(8,128)} %slice.347) | copy-start | bytes 552964
  496.6 31.4 %copy-start.26 = (f32[8,45,128]{2,1,0:T(8,128)S(1)}, f32[8,45,128]{2,1,0:T(8,128)}, u32[]{:S(2)}) copy-start(f32[8,45,128]{2,1,0:T(8,128)} %slice.349) | copy-start | bytes 552964
  499.2 43.4 %collective-permute-start.10 = (f32[8,1,256]{2,1,0:T(1,128)}, f32[8,1,256]{2,1,0:T(1,128)}, u32[]{:S(2)}, u32[]{:S(2)}) collective-permute-start(f32[8,1,256]{2,1,0:T(1,128)} %slice.485), channel_id=1, source_target_pairs={{1,0},{3,2},{5,4},{7,6},{9,8},{11,10},{13,12},{15,14},{17,16},{19,... | collective-permute-start | bytes 24584 | tf_op jit(solution)/shard_map/ppermute | solution.py:29
  503.5 25.6 %copy-start.34 = (f32[8,45,128]{2,1,0:T(8,128)S(1)}, f32[8,45,128]{2,1,0:T(8,128)}, u32[]{:S(2)}) copy-start(f32[8,45,128]{2,1,0:T(8,128)} %slice.351) | copy-start | bytes 552964
  542.6 8.2 copy-start.123
  543.3 6.7 collective-permute-start.11
  555.0 126.7 %copy-start.89 = (f32[64,64]{1,0:T(8,128)S(1)}, f32[64,64]{1,0:T(8,128)}, u32[]{:S(2)}) copy-start(f32[64,64]{1,0:T(8,128)} %param.58) | copy-start | bytes 49156
  558.0 126.5 %copy-start.83 = (f32[64,64]{1,0:T(8,128)S(1)}, f32[64,64]{1,0:T(8,128)}, u32[]{:S(2)}) copy-start(f32[64,64]{1,0:T(8,128)} %param.59) | copy-start | bytes 49156
  558.0 140.0 %copy-start.70 = (f32[256,256]{1,0:T(8,128)S(1)}, f32[256,256]{1,0:T(8,128)}, u32[]{:S(2)}) copy-start(f32[256,256]{1,0:T(8,128)} %param.43) | copy-start | bytes 786436
  681.7 16.2 %copy-start.14 = (f32[1152,256]{1,0:T(8,128)S(1)}, f32[1152,256]{1,0:T(8,128)}, u32[]{:S(2)}) copy-start(f32[1152,256]{1,0:T(8,128)} %get-tuple-element.201) | copy-start | bytes 3538948
  684.5 15.5 %copy-start.78 = (f32[64,64]{1,0:T(8,128)}, f32[64,64]{1,0:T(8,128)S(1)}, u32[]{:S(2)}) copy-start(f32[64,64]{1,0:T(8,128)S(1)} %fusion.165) | copy-start | bytes 49156
  685.0 15.0 %copy-start.21 = (f32[256,256]{1,0:T(8,128)S(1)}, f32[256,256]{1,0:T(8,128)}, u32[]{:S(2)}) copy-start(f32[256,256]{1,0:T(8,128)} %param.44) | copy-start | bytes 786436
  708.3 54.4 %copy-start.152 = (s32[2]{0:T(128)S(1)}, s32[2]{0:T(128)}, u32[]{:S(2)}) copy-start(s32[2]{0:T(128)} %iota_multiply_fusion) | copy-start | bytes 28
  842.1 33.3 %copy-start.18 = (f32[256,256]{1,0:T(8,128)S(1)}, f32[256,256]{1,0:T(8,128)}, u32[]{:S(2)}) copy-start(f32[256,256]{1,0:T(8,128)} %fusion.386) | copy-start | bytes 786436
  938.9 7.0 copy-start.20
  (107 other events, 335.2 us)
Sparse Core Ops, SparseCore 0:
  10.9 58.9 all-gather.4
  72.6 54.1 all-gather.6
  129.6 58.7 all-gather.8
  539.5 142.1 all-reduce.9
where the time goes:
time: 967 us; the launch traced here: 958 us
  other arithmetic  240 us (25%)
  blocking collectives  235 us (24%)
  matrix products  188 us (19%)
  waiting for transfers between devices  176 us (18%)
  local copies, waits for them, and re-layouts  75.5 us (8%)
  starting transfers between devices  23.8 us (2%)
  between operations  20.3 us (2%)
    another operation x27, other arithmetic, soap_step(): factor = jnp.linalg.cholesky(matmul(product.T, product))  130 us
    psum x1, waiting for transfers between devices, local(): lax.psum((grad_down, grad_upward, grad_lateral, grad_merging, grad_heads,...  124 us
    psum x3, blocking collectives, norm_backward(): lax.psum((jnp.sum(grad_hidden * normed, axis=(0, 1)), jnp.sum(grad_hidden...  118 us
    psum x3, blocking collectives, norm_forward(): lax.psum((jnp.sum(feature, axis=(0, 1)), jnp.sum(feature * feature, axis=...  117 us
    another operation x11, other arithmetic, soap_step(): jax.scipy.linalg.solve_triangular(factor, product.T, lower=True)  80.2 us
    dot_general x44, matrix products, matmul(): jnp.dot(left, right, precision=HIGHEST, preferred_element_type=jnp.float32)  64.1 us
    dot_general x24, matrix products, contract(): return jnp.tensordot(left, right, axes=((0, 1), (0, 1)), precision=HIGHEST)  49 us
    dot_general x24, matrix products, back_product(): return jnp.tensordot(upstream, matrix, axes=((2,), (1,)), precision=HIGHEST)  46.6 us
  transfers between devices with their start and end apart: 16, of which 6 were waited for; matrix products, arithmetic and copies ran while one was open for 13% of the time, Pallas kernels for 0%

commit v1 on v0

--- a/solution.py
+++ b/solution.py
@@ -1,8 +1,11 @@
+import functools
 import math
 
 import jax
 import jax.numpy as jnp
 from jax import lax
+from jax.experimental import pallas as pl
+from jax.experimental.pallas import tpu as pltpu
 from jax.sharding import PartitionSpec as P
 
 C0 = 128
@@ -21,6 +24,127 @@
 DECAY = 0.01
 VECTOR_RATE = 0.1
 HIGHEST = lax.Precision.HIGHEST
+
+
+F32=jnp.float32
+def dot(a,b,ca,cb):
+    return lax.dot_general(a,b,(((ca,),(cb,)),((),())),precision=HIGHEST,preferred_element_type=F32)
+NB=32
+def base_inverse(blocks):
+    lane=lax.broadcasted_iota(jnp.int32,(NB,128),1); row=lax.broadcasted_iota(jnp.int32,(NB,128),0)
+    eye=(lane==row+NB).astype(F32)
+    xs=[jnp.concatenate([b,jnp.zeros((NB,128-NB),F32)],axis=1)+eye for b in blocks]
+    for k in range(NB):
+        nx=[]
+        for x in xs:
+            col=jnp.broadcast_to(x[:,k:k+1],(NB,128))
+            piv=col[k:k+1,:]
+            r=x[k:k+1,:]*(1.0/piv)
+            nx.append(x-jnp.where(row>k,col,0.0)*r)
+        xs=nx
+    outs=[]
+    for x in xs:
+        d=jnp.sum(jnp.where(lane==row,x,0.0),axis=1,keepdims=True)
+        y=x*lax.rsqrt(d)
+        outs.append(y[:,NB:2*NB])
+    return outs
+def kern(ns,*refs):
+    m=len(ns)
+    gram=refs[0:m]; add=refs[m:2*m]; basis=refs[2*m:3*m]
+    out_gram=refs[3*m:4*m]; out_rot=refs[4*m:5*m]
+    aa=refs[5*m:6*m]; xx=refs[6*m:7*m]
+    prods=[]
+    for i,n in enumerate(ns):
+        g=0.95*gram[i][...]+0.05*add[i][...]
+        out_gram[i][...]=g
+        p=dot(g,basis[i][...],1,0)
+        out_rot[i][...]=p
+        a=dot(p,p,0,0)
+        npad=aa[i].shape[0]
+        if npad!=n:
+            r=lax.broadcasted_iota(jnp.int32,(npad,npad),0); c=lax.broadcasted_iota(jnp.int32,(npad,npad),1)
+            aa[i][...]=((r==c)&(r>=n)).astype(F32)
+            aa[i][0:n,0:n]=a
+        else:
+            aa[i][...]=a
+        r=lax.broadcasted_iota(jnp.int32,(npad,npad),0); c=lax.broadcasted_iota(jnp.int32,(npad,npad),1)
+        xx[i][...]=(r==c).astype(F32)
+    for b in range(max(a.shape[0] for a in aa)//NB):
+        s=b*NB
+        live=[i for i in range(m) if s<aa[i].shape[0]]
+        inv=base_inverse([aa[i][s:s+NB,s:s+NB] for i in live])
+        for i,li in zip(live,inv):
+            npad=aa[i].shape[0]
+            e=s+NB
+            y=dot(li,xx[i][s:e,:],1,0)
+            xx[i][s:e,:]=y
+            if e<npad:
+                rpan=dot(li,aa[i][s:e,e:],1,0)
+                cpan=dot(aa[i][e:,s:e],li,1,1)
+                aa[i][e:,e:]=aa[i][e:,e:]-dot(cpan,rpan,1,0)
+                xx[i][e:,:]=xx[i][e:,:]-dot(cpan,y,1,0)
+    for i,n in enumerate(ns):
+        out_rot[i][...]=dot(out_rot[i][...],xx[i][0:n,0:n],1,1)
+def rotations(grams,adds,bases):
+    ns=[g.shape[0] for g in grams]
+    pads=[-(-n//NB)*NB for n in ns]
+    outs=pl.pallas_call(functools.partial(kern,ns),
+        out_shape=[jax.ShapeDtypeStruct((n,n),F32) for n in ns]*2,
+        scratch_shapes=[pltpu.VMEM((p,p),F32) for p in pads]*2,
+        compiler_params=pltpu.CompilerParams(vmem_limit_bytes=32<<20),
+        name='rotate')(*grams,*adds,*bases)
+    return outs[:len(ns)],outs[len(ns):]
+
+
+def exchange(value):
+    return lax.ppermute(value, "stream", [(0, 1), (1, 0)])
+
+
+def everyone(value, axes):
+    count = lax.axis_size(axes)
+    copies = jnp.broadcast_to(value[None], (count,) + value.shape)
+    return lax.all_to_all(copies, axes, 0, 0, tiled=True)
+
+
+def sum_small(pieces):
+    flat = jnp.concatenate([piece.reshape(-1) for piece in pieces])
+    total = jnp.sum(everyone(flat, ("dp", "stream")), axis=0)
+    out = []
+    offset = 0
+    for piece in pieces:
+        out.append(total[offset : offset + piece.size].reshape(piece.shape))
+        offset += piece.size
+    return out
+
+
+def join_halves(mine, axis):
+    other = exchange(mine)
+    first = lax.axis_index("stream") == 0
+    return jnp.concatenate(
+        [jnp.where(first, mine, other), jnp.where(first, other, mine)], axis=axis
+    )
+
+
+def own_half(value, axis, which):
+    half = value.shape[axis] // 2
+    return lax.dynamic_slice_in_dim(value, which * half, half, axis)
+
+
+def gather_rows(shard, axis):
+    mine = own_half(shard, axis, lax.axis_index("stream"))
+    blocks = everyone(mine, "dp")
+    if axis == 1:
+        return join_halves(blocks.reshape(-1, mine.shape[1]), 1)
+    joined = join_halves(blocks, 1)
+    return joined.reshape(-1, shard.shape[1])
+
+
+def scatter_half(full, axis):
+    core = lax.axis_index("stream")
+    count = lax.axis_size("dp")
+    blocks = full.reshape((count, full.shape[0] // count) + full.shape[1:])
+    mine = own_half(blocks, axis + 1, core) + exchange(own_half(blocks, axis + 1, 1 - core))
+    return jnp.sum(lax.all_to_all(mine, "dp", 0, 0, tiled=True), axis=0)
 
 
 def from_behind(block, axis, distance):
@@ -64,6 +188,17 @@
     return jnp.tensordot(gradient, gradient, axes=((0,), (0,)), precision=HIGHEST)
 
 
+def contract_rows(left, right):
+    return jnp.tensordot(left, right, axes=((0,), (0,)), precision=HIGHEST)
+
+
+def all_halves(partial, axis):
+    count = lax.axis_size("dp")
+    blocks = partial.reshape((count, partial.shape[0] // count) + partial.shape[1:])
+    mine = jnp.sum(lax.all_to_all(blocks, "dp", 0, 0, tiled=True), axis=0)
+    return join_halves(everyone(mine, "dp").reshape(partial.shape), axis)
+
+
 def keep_rows(global_rows, total_rows):
     wrapped = jnp.remainder(global_rows, total_rows)
     return ((wrapped + SCENE_ROWS // 2) % SCENE_ROWS != 0).astype(jnp.float32)
@@ -91,8 +226,8 @@
 
 
 def norm_forward(feature, norm_gain, norm_shift, pixels):
-    totals = lax.psum(
-        (jnp.sum(feature, axis=(0, 1)), jnp.sum(feature * feature, axis=(0, 1))), ("dp", "stream")
+    totals = sum_small(
+        (jnp.sum(feature, axis=(0, 1)), jnp.sum(feature * feature, axis=(0, 1)))
     )
     centre = totals[0] / pixels
     spread = lax.rsqrt(totals[1] / pixels - centre * centre + EPS_NORM)
@@ -104,9 +239,8 @@
     hidden = norm_gain * normed + norm_shift
     sigmoid = jax.nn.sigmoid(hidden)
     grad_hidden = upstream * sigmoid * (1.0 + hidden * (1.0 - sigmoid))
-    grad_gain, grad_shift = lax.psum(
-        (jnp.sum(grad_hidden * normed, axis=(0, 1)), jnp.sum(grad_hidden, axis=(0, 1))),
-        ("dp", "stream"),
+    grad_gain, grad_shift = sum_small(
+        (jnp.sum(grad_hidden * normed, axis=(0, 1)), jnp.sum(grad_hidden, axis=(0, 1)))
     )
     grad_feature = (
         norm_gain * spread * (grad_hidden - grad_shift / pixels - normed * (grad_gain / pixels))
@@ -123,7 +257,7 @@
     return (params - VECTOR_RATE * (direction + DECAY * params), momentum, variance)
 
 
-def soap_step(weight, moment, square, gram_old, basis_old, gradient, gram_sum, step_rate):
+def soap_step(weight, moment, square, basis_old, gradient, step_rate):
     rotated = matmul(gradient, basis_old)
     momentum = BETA_ONE * moment + (1.0 - BETA_ONE) * rotated
     variance = BETA_TWO * square + (1.0 - BETA_TWO) * rotated * rotated
@@ -131,11 +265,7 @@
         momentum / (1.0 - BETA_ONE**STEP) / (jnp.sqrt(variance / (1.0 - BETA_TWO**STEP)) + EPS_ADAM)
     )
     renewed = weight - step_rate * (matmul(direction, basis_old.T) + DECAY * weight)
-    gramian = BETA_GRAM * gram_old + (1.0 - BETA_GRAM) * gram_sum
-    product = matmul(gramian, basis_old)
-    factor = jnp.linalg.cholesky(matmul(product.T, product))
-    rotation = jax.scipy.linalg.solve_triangular(factor, product.T, lower=True).T
-    return (renewed, momentum, variance, gramian, rotation)
+    return (renewed, momentum, variance)
 
 
 def local(
@@ -184,9 +314,9 @@
         [left_live[None], jnp.ones((breadth,), jnp.float32), right_live[None]]
     )[None, :, None]
     down_full, upward_full, merging_full = (
-        lax.all_gather(down_weight, "dp", axis=0, tiled=True),
-        lax.all_gather(upward_weight, "dp", axis=0, tiled=True),
-        lax.all_gather(merging_weight, "dp", axis=0, tiled=True),
+        gather_rows(down_weight, 1),
+        gather_rows(upward_weight, 1),
+        gather_rows(merging_weight, 0),
     )
     (
         gain_one,
@@ -353,23 +483,18 @@
         back_quads.append(quad_row)
     grad_masked = grad_masked + assemble_quads(back_quads)
     feats_grad = grad_masked * occupancy
-    dp_index = lax.axis_index("dp")
-    total_down, total_upward, total_lateral, total_merging, total_heads, total_bias = lax.psum(
-        (grad_down, grad_upward, grad_lateral, grad_merging, grad_heads, grad_bias),
-        ("dp", "stream"),
-    )
-    down_shard = lax.dynamic_slice_in_dim(
-        total_down, dp_index * down_weight.shape[0], down_weight.shape[0], 0
-    )
-    upward_shard = lax.dynamic_slice_in_dim(
-        total_upward, dp_index * upward_weight.shape[0], upward_weight.shape[0], 0
-    )
-    merging_shard = lax.dynamic_slice_in_dim(
-        total_merging, dp_index * merging_weight.shape[0], merging_weight.shape[0], 0
-    )
-    gram_down = gram_rows(total_down)
-    gram_upward = gram_rows(total_upward)
-    gram_merging = gram_rows(total_merging)
+    down_shard = join_halves(scatter_half(grad_down, 1), 1)
+    upward_shard = join_halves(scatter_half(grad_upward, 1), 1)
+    merging_shard = join_halves(scatter_half(grad_merging, 0), 0)
+    core = lax.axis_index("stream")
+    partial_down = contract_rows(down_shard, own_half(down_shard, 1, core))
+    partial_upward = contract_rows(upward_shard, own_half(upward_shard, 1, core))
+    gram_down = all_halves(partial_down, 1)
+    gram_upward = all_halves(partial_upward, 1)
+    total_lateral = join_halves(everyone(scatter_half(grad_lateral, 1), "dp").reshape(C0, C1 // 2), 1)
+    total_heads, total_bias, gram_merging = sum_small(
+        (grad_heads, grad_bias, gram_rows(merging_shard) * 0.5)
+    )
     grad_vector = jnp.concatenate(
         [
             gain_grad_one,
@@ -386,59 +511,49 @@
     vector_renewed, vector_momentum, vector_variance = adam_vector(
         vector_params, vector_moment, vector_square, grad_vector
     )
-    down_renewed, down_momentum, down_variance, down_gramian, down_rotation = soap_step(
-        down_weight,
-        down_moment,
-        down_square,
-        down_gram,
-        down_basis,
-        down_shard,
-        gram_down,
-        1.0 / math.sqrt(9 * C0),
-    )
-    upward_renewed, upward_momentum, upward_variance, upward_gramian, upward_rotation = soap_step(
+    down_renewed, down_momentum, down_variance = soap_step(
+        down_weight, down_moment, down_square, down_basis, down_shard, 1.0 / math.sqrt(9 * C0)
+    )
+    upward_renewed, upward_momentum, upward_variance = soap_step(
         upward_weight,
         upward_moment,
         upward_square,
-        upward_gram,
         upward_basis,
         upward_shard,
-        gram_upward,
         1.0 / math.sqrt(C1),
     )
-    lateral_renewed, lateral_momentum, lateral_variance, lateral_gramian, lateral_rotation = (
-        soap_step(
-            lateral_weight,
-            lateral_moment,
-            lateral_square,
-            lateral_gram,
-            lateral_basis,
-            total_lateral,
+    lateral_renewed, lateral_momentum, lateral_variance = soap_step(
+        lateral_weight,
+        lateral_moment,
+        lateral_square,
+        lateral_basis,
+        total_lateral,
+        1.0 / math.sqrt(C0),
+    )
+    merging_renewed, merging_momentum, merging_variance = soap_step(
+        merging_weight,
+        merging_moment,
+        merging_square,
+        merging_basis,
+        merging_shard,
+        1.0 / math.sqrt(18 * C1),
+    )
+    heads_renewed, heads_momentum, heads_variance = soap_step(
+        heads_weight, heads_moment, heads_square, heads_basis, total_heads, 1.0 / math.sqrt(C2)
+    )
+    (
+        (down_gramian, upward_gramian, lateral_gramian, merging_gramian, heads_gramian),
+        (down_rotation, upward_rotation, lateral_rotation, merging_rotation, heads_rotation),
+    ) = rotations(
+        (down_gram, upward_gram, lateral_gram, merging_gram, heads_gram),
+        (
+            gram_down,
+            gram_upward,
             gram_rows(total_lateral),
-            1.0 / math.sqrt(C0),
-        )
-    )
-    merging_renewed, merging_momentum, merging_variance, merging_gramian, merging_rotation = (
-        soap_step(
-            merging_weight,
-            merging_moment,
-            merging_square,
-            merging_gram,
-            merging_basis,
-            merging_shard,
             gram_merging,
-            1.0 / math.sqrt(18 * C1),
-        )
-    )
-    heads_renewed, heads_momentum, heads_variance, heads_gramian, heads_rotation = soap_step(
-        heads_weight,
-        heads_moment,
-        heads_square,
-        heads_gram,
-        heads_basis,
-        total_heads,
-        gram_rows(total_heads),
-        1.0 / math.sqrt(C2),
+            gram_rows(total_heads),
+        ),
+        (down_basis, upward_basis, lateral_basis, merging_basis, heads_basis),
     )
     return (
         head_maps,

time: 967 us -> 594 us (0.61)
  blocking collectives: 235 us -> 0 us
  other arithmetic: 240 us -> 47.3 us
  starting transfers between devices: 23.8 us -> 124 us
  waiting for transfers between devices: 176 us -> 134 us
  Pallas kernels: 0 us -> 37.1 us
  matrix products: 188 us -> 157 us
  between operations: 20.3 us -> 4.31 us
    psum x6 -> x0, blocking collectives: 235 us -> none  [the longest x3 118 us: norm_backward(): lax.psum((jnp.sum(grad_hidden * normed, axis=(0, 1)), jnp.sum(grad_hidden...]
    another operation x38 -> x0, other arithmetic: 210 us -> none  [the longest x27 130 us: soap_step(): factor = jnp.linalg.cholesky(matmul(product.T, product))]
    psum x1 -> x0, waiting for transfers between devices: 124 us -> none  [local(): lax.psum((grad_down, grad_upward, grad_lateral, grad_merging, grad_heads,...]
    all_to_all x0 -> x21, waiting for transfers between devices: none -> 123 us  [the longest x15 94 us: everyone(): return lax.all_to_all(copies, axes, 0, 0, tiled=True)]
    all_to_all x0 -> x21, starting transfers between devices: none -> 99 us  [the longest x15 68.1 us: everyone(): return lax.all_to_all(copies, axes, 0, 0, tiled=True)]
    all_gather x3 -> x0, waiting for transfers between devices: 42.2 us -> none  [the longest x1 31.4 us: local(): lax.all_gather(down_weight, 'dp', axis=0, tiled=True)]
    pallas_call x0 -> x1, Pallas kernels: none -> 37.1 us  [rotations(): pl.pallas_call(functools.partial(kern, ns), out_shape=[jax.ShapeDtypeStru...]
    another operation x28 -> x0, local copies, waits for them, and re-layouts: 22.4 us -> none  [the longest x22 19.3 us: soap_step(): jax.scipy.linalg.solve_triangular(factor, product.T, lower=True)]
  transfers between devices with their start and end apart: 16 -> 46, of which waited for: 6 -> 23; matrix products, arithmetic and copies ran while one was open for 13% -> 25% of each run, Pallas kernels for 0% -> 0%
where the time goes in v1:
time: 594 us; the launch traced here: 583 us
  matrix products  157 us (26%)
  waiting for transfers between devices  134 us (23%)
  starting transfers between devices  124 us (21%)
  local copies, waits for them, and re-layouts  79 us (13%)
  other arithmetic  47.3 us (8%)
  Pallas kernels  37.1 us (6%)
    all_to_all x15, waiting for transfers between devices, everyone(): return lax.all_to_all(copies, axes, 0, 0, tiled=True)  94 us
    all_to_all x15, starting transfers between devices, everyone(): return lax.all_to_all(copies, axes, 0, 0, tiled=True)  68.1 us
    dot_general x34, matrix products, matmul(): jnp.dot(left, right, precision=HIGHEST, preferred_element_type=jnp.float32)  64.4 us
    dot_general x24, matrix products, back_product(): return jnp.tensordot(upstream, matrix, axes=((2,), (1,)), precision=HIGHEST)  51.1 us
    dot_general x24, matrix products, contract(): return jnp.tensordot(left, right, axes=((0, 1), (0, 1)), precision=HIGHEST)  38.6 us
    pallas_call x1, Pallas kernels, rotations(): pl.pallas_call(functools.partial(kern, ns), out_shape=[jax.ShapeDtypeStru...  37.1 us
    all_to_all x4, starting transfers between devices, scatter_half(): return jnp.sum(lax.all_to_all(mine, 'dp', 0, 0, tiled=True), axis=0)  21.5 us
    unnamed x373, local copies, waits for them, and re-layouts  20.4 us
  transfers between devices with their start and end apart: 46, of which 23 were waited for; matrix products, arithmetic and copies ran while one was open for 25% of the time, Pallas kernels for 0%

profile of v1, /device:TPU:0, one launch (start us, length us, event | category | flops | bytes accessed | tf_op | source)
XLA Modules:
  0.0 582.7 jit_solution(17047240877510618751)
XLA Ops:
  2.4 8.4 %all-to-all-start = ((f32[16,72,128]{2,1,0:T(8,128)}), f32[16,72,128]{2,1,0:T(8,128)}, u32[]{:S(2)}, u32[]{:S(2)}) async-start(f32[16,72,128]{2,1,0:T(8,128)} %broadcast_in_dim.42), calls=%async_computation | async-start | bytes 1179648 | tf_op jit(solution)/shard_map/all_to_all | solution.py:106
  14.8 12.3 %all-to-all-done = f32[16,72,128]{2,1,0:T(8,128)} async-done(((f32[16,72,128]{2,1,0:T(8,128)}), f32[16,72,128]{2,1,0:T(8,128)}, u32[]{:S(2)}, u32[]{:S(2)}) %all-to-all-start) | async-done | bytes 589856 | tf_op jit(solution)/shard_map/all_to_all | solution.py:106
  27.9 4.2 all-to-all-start.2
  58.9 3.9 all-to-all-start.1
  64.8 5.3 all-to-all-done.1
  81.9 5.0 all-to-all-start.5
  89.8 21.8 %all-to-all-done.5 = f32[16,144,64]{1,2,0:T(8,128)} async-done(((f32[16,144,64]{1,2,0:T(8,128)}), f32[16,144,64]{1,2,0:T(8,128)}, u32[]{:S(2)}, u32[]{:S(2)}) %all-to-all-start.5) | async-done | bytes 589856 | tf_op jit(solution)/shard_map/all_to_all | solution.py:106
  112.3 5.1 all-to-all-start.3
  127.3 5.0 collective-permute-start.5
  134.0 3.3 collective-permute-done.4
  145.3 3.8 fusion.30
  149.1 3.8 fusion.26
  153.0 3.7 fusion.22
  156.6 12.6 %fusion.18 = f32[16,90,64]{1,2,0:T(8,128)S(1)} fusion(f32[18,92,512]{2,1,0:T(8,128)S(1)} %maximum_multiply_fusion, f32[4608,64]{0,1:T(8,128)S(1)} %copy-done.30), kind=kOutput, calls=%fused_computation.20 | convolution fusion | flops 566231040 | bytes 3645440 | tf_op jit(solution)/shard_map/dot_general | solution.py:176
  169.2 3.8 fusion.14
  173.0 3.7 fusion.47
  176.7 3.8 fusion.50
  180.5 4.2 fusion.53
  184.7 4.7 fusion.405
  190.1 5.1 all-to-all-start.6
  198.4 3.8 all-to-all-done.6
  204.8 3.2 multiply_reduce_fusion.4
  208.8 3.2 all-to-all-start.7
  212.0 2.9 convolution_add_fusion.1
  232.4 2.8 fusion.126
  240.2 5.4 collective-permute-start.10
  248.4 4.8 collective-permute-done.9
  258.8 4.4 fusion.150
  263.2 3.7 reshape.336
  272.8 3.2 fusion.176
  276.1 3.2 fusion.178
  279.3 3.2 fusion.172
  282.5 3.4 fusion.170
  288.7 4.9 fusion.166
  293.6 4.9 fusion.164
  298.5 5.7 add_add_fusion
  304.4 2.9 multiply_reduce_fusion.1
  310.6 3.5 constant_dynamic-slice_fusion.4
  318.6 4.0 all-to-all-start.8
  322.8 2.9 subtract_multiply_fusion
  333.9 3.1 convolution_bitcast_fusion.5
  345.7 5.7 all-to-all-start.10
  352.9 5.9 %all-to-all-done.10 = f32[32,1,512]{2,1,0:T(1,128)S(1)} async-done(((f32[32,1,512]{2,1,0:T(1,128)}), f32[32,1,512]{2,1,0:T(1,128)S(1)}, u32[]{:S(2)}, u32[]{:S(2)}) %all-to-all-start.10) | async-done | bytes 65568 | tf_op jit(solution)/shard_map/all_to_all | solution.py:106
  358.8 3.9 all-to-all-start.19
  372.4 6.9 %all-to-all-start.20 = ((f32[16,8,128]{2,1,0:T(8,128)}), f32[16,8,128]{2,1,0:T(8,128)}, u32[]{:S(2)}, u32[]{:S(2)}) async-start(f32[16,8,128]{2,1,0:T(8,128)} %broadcast_in_dim.61), calls=%async_computation.20 | async-start | bytes 131072 | tf_op jit(solution)/shard_map/all_to_all | solution.py:106
  381.3 5.5 all-to-all-done.20
  386.9 4.2 all-to-all-start.16
  400.6 5.1 all-to-all-done.16
  405.8 4.3 all-to-all-start.13
  411.3 5.5 collective-permute-start.14
  421.5 2.8 copy_add_fusion
  425.4 9.1 %all-to-all-start.11 = ((f32[16,144,64]{1,2,0:T(8,128)}), f32[16,144,64]{1,2,0:T(8,128)}, u32[]{:S(2)}, u32[]{:S(2)}) async-start(f32[16,144,64]{1,2,0:T(8,128)} %copy_add_fusion), calls=%async_computation.11 | async-start | bytes 2097152 | tf_op jit(solution)/shard_map/all_to_all | solution.py:147
  444.0 13.9 %all-to-all-done.11 = f32[16,144,64]{1,2,0:T(8,128)} async-done(((f32[16,144,64]{1,2,0:T(8,128)}), f32[16,144,64]{1,2,0:T(8,128)}, u32[]{:S(2)}, u32[]{:S(2)}) %all-to-all-start.11) | async-done | bytes 589856 | tf_op jit(solution)/shard_map/all_to_all | solution.py:147
  457.9 5.8 all-to-all-start.17
  465.6 5.9 %all-to-all-done.17 = f32[16,16,128]{2,1,0:T(8,128)S(1)} async-done(((f32[16,16,128]{2,1,0:T(8,128)}), f32[16,16,128]{2,1,0:T(8,128)S(1)}, u32[]{:S(2)}, u32[]{:S(2)}) %all-to-all-start.17) | async-done | bytes 131104 | tf_op jit(solution)/shard_map/all_to_all | solution.py:198
  472.2 3.5 all-to-all-start.14
  475.7 2.9 fusion.40
  484.1 4.3 all-to-all-start.18
  491.4 4.8 all-to-all-done.18
  496.9 3.5 all-to-all-start.15
  500.9 7.3 %all-to-all-done.15 = f32[16,16,128]{2,1,0:T(8,128)S(1)} async-done(((f32[16,16,128]{2,1,0:T(8,128)}), f32[16,16,128]{2,1,0:T(8,128)S(1)}, u32[]{:S(2)}, u32[]{:S(2)}) %all-to-all-start.15) | async-done | bytes 131104 | tf_op jit(solution)/shard_map/all_to_all | solution.py:106
  509.8 3.7 all-to-all-start.12
  519.6 21.3 %all-to-all-done.12 = f32[32,1,8646]{2,1,0:T(1,128)} async-done(((f32[32,1,8646]{2,1,0:T(1,128)}), f32[32,1,8646]{2,1,0:T(1,128)}, u32[]{:S(2)}, u32[]{:S(2)}) %all-to-all-start.12) | async-done | bytes 1106720 | tf_op jit(solution)/shard_map/all_to_all | solution.py:106
  545.1 37.1 %rotate.1 = (f32[256,256]{1,0:T(8,128)}, f32[256,256]{1,0:T(8,128)}, f32[256,256]{1,0:T(8,128)}, f32[64,64]{1,0:T(8,128)}, f32[70,70]{1,0:T(8,128)}, /*index=5*/...) custom-call(f32[256,256]{1,0:T(8,128)S(1)} %copy-done.3, ...), custom_call_target="tpu_custom_call" | custom-call | tf_op jit(solution)/shard_map/rotate/pallas_call | solution.py:91
  (631 shorter events, 202.7 us)
Async XLA Ops:
  2.4 24.7 %all-to-all-start = ((f32[16,72,128]{2,1,0:T(8,128)}), f32[16,72,128]{2,1,0:T(8,128)}, u32[]{:S(2)}, u32[]{:S(2)}) async-start(f32[16,72,128]{2,1,0:T(8,128)} %broadcast_in_dim.42), calls=%async_computation | async-start | bytes 1179648 | tf_op jit(solution)/shard_map/all_to_all | solution.py:106
  11.1 30.4 %collective-permute-start = (f32[16,1,128]{2,1,0:T(1,128)S(1)}, f32[16,1,128]{2,1,0:T(1,128)S(1)}, u32[]{:S(2)}, u32[]{:S(2)}) collective-permute-start(f32[16,1,128]{2,1,0:T(1,128)S(1)} %slice.440), channel_id=1, source_target_pairs={{0,1},{2,3},{4,5},{6,7},{8,9},{10,11},{12,13},{14,15},{16,17},{18,... | collective-permute-start | bytes 24584 | tf_op jit(solution)/shard_map/ppermute | solution.py:153
  14.7 111.3 %copy-start.16 = (f32[16,90,256]{2,1,0:T(8,128)}, f32[16,90,256]{2,1,0:T(8,128)S(1)}, u32[]{:S(2)}) copy-start(f32[16,90,256]{2,1,0:T(8,128)S(1)} %get-tuple-element.296) | copy-start | bytes 4423684
  27.9 22.3 %all-to-all-start.2 = ((f32[16,64,128]{2,1,0:T(8,128)}), f32[16,64,128]{2,1,0:T(8,128)}, u32[]{:S(2)}, u32[]{:S(2)}) async-start(f32[16,64,128]{2,1,0:T(8,128)} %broadcast_in_dim.44), calls=%async_computation.2 | async-start | bytes 1048576 | tf_op jit(solution)/shard_map/all_to_all | solution.py:106
  32.9 17.4 %collective-permute-start.2 = (f32[1152,128]{1,0:T(8,128)}, f32[1152,128]{1,0:T(8,128)}, u32[]{:S(2)}, u32[]{:S(2)}) collective-permute-start(f32[1152,128]{1,0:T(8,128)} %bitcast), channel_id=1, source_target_pairs={{0,1},{1,0},{2,3},{3,2},{4,5},{5,4},{6,7},{7,6},{8,9},{9,8},{10,11... | collective-permute-start | bytes 1769480 | tf_op jit(solution)/shard_map/ppermute | solution.py:100
  41.5 7.9 %collective-permute-start.1 = (f32[1,91,128]{2,1,0:T(8,128)S(1)}, f32[1,91,128]{2,1,0:T(8,128)S(1)}, u32[]{:S(2)}, u32[]{:S(2)}) collective-permute-start(f32[1,91,128]{2,1,0:T(8,128)S(1)} %fusion.275), channel_id=1, source_target_pairs={{0,2},{2,4},{4,6},{6,8},{8,10},{10,12},{12,14},{14,16},{16,18},{18... | collective-permute-start | bytes 139784 | tf_op jit(solution)/shard_map/ppermute | solution.py:159
  50.2 12.6 %collective-permute-start.3 = (f32[1024,128]{1,0:T(8,128)}, f32[1024,128]{1,0:T(8,128)}, u32[]{:S(2)}, u32[]{:S(2)}) collective-permute-start(f32[1024,128]{1,0:T(8,128)} %bitcast.10), channel_id=1, source_target_pairs={{0,1},{1,0},{2,3},{3,2},{4,5},{5,4},{6,7},{7,6},{8,9},{9,8},{10,11... | collective-permute-start | bytes 1572872 | tf_op jit(solution)/shard_map/ppermute | solution.py:100
  58.2 29.4 %copy-start.57 = (f32[8,45,256]{2,1,0:T(8,128)}, f32[8,45,256]{2,1,0:T(8,128)S(1)}, u32[]{:S(2)}) copy-start(f32[8,45,256]{2,1,0:T(8,128)S(1)} %get-tuple-element.297) | copy-start | bytes 1105924
  58.9 11.3 %all-to-all-start.1 = ((f32[32,1,512]{2,1,0:T(1,128)}), f32[32,1,512]{2,1,0:T(1,128)S(1)}, u32[]{:S(2)}, u32[]{:S(2)}) async-start(f32[32,1,512]{2,1,0:T(1,128)} %broadcast_in_dim.43), calls=%async_computation.1 | async-start | bytes 131072 | tf_op jit(solution)/shard_map/all_to_all | solution.py:106
  70.8 10.0 %all-to-all-start.4 = ((f32[32,1,512]{2,1,0:T(1,128)}), f32[32,1,512]{2,1,0:T(1,128)S(1)}, u32[]{:S(2)}, u32[]{:S(2)}) async-start(f32[32,1,512]{2,1,0:T(1,128)} %broadcast_in_dim.46), calls=%async_computation.4 | async-start | bytes 131072 | tf_op jit(solution)/shard_map/all_to_all | solution.py:106
  81.9 29.7 %all-to-all-start.5 = ((f32[16,144,64]{1,2,0:T(8,128)}), f32[16,144,64]{1,2,0:T(8,128)}, u32[]{:S(2)}, u32[]{:S(2)}) async-start(f32[16,144,64]{1,2,0:T(8,128)} %broadcast_in_dim.52), calls=%async_computation.5 | async-start | bytes 2097152 | tf_op jit(solution)/shard_map/all_to_all | solution.py:106
  112.3 12.5 %all-to-all-start.3 = ((f32[32,1,512]{2,1,0:T(1,128)}), f32[32,1,512]{2,1,0:T(1,128)S(1)}, u32[]{:S(2)}, u32[]{:S(2)}) async-start(f32[32,1,512]{2,1,0:T(1,128)} %broadcast_in_dim.45), calls=%async_computation.3 | async-start | bytes 131072 | tf_op jit(solution)/shard_map/all_to_all | solution.py:106
  118.6 13.7 %collective-permute-start.8 = (f32[16,144,64]{1,2,0:T(8,128)}, f32[16,144,64]{1,2,0:T(8,128)}, u32[]{:S(2)}, u32[]{:S(2)}) collective-permute-start(f32[16,144,64]{1,2,0:T(8,128)} %all-to-all-done.5), channel_id=1, source_target_pairs={{0,1},{1,0},{2,3},{3,2},{4,5},{5,4},{6,7},{7,6},{8,9},{9,8},{10,11... | collective-permute-start | bytes 1769480 | tf_op jit(solution)/shard_map/ppermute | solution.py:100
  126.6 10.7 %collective-permute-start.4 = (f32[1,90,512]{2,1,0:T(8,128)S(1)}, f32[1,90,512]{2,1,0:T(8,128)S(1)}, u32[]{:S(2)}, u32[]{:S(2)}) collective-permute-start(f32[1,90,512]{2,1,0:T(8,128)S(1)} %get-tuple-element.226), channel_id=1, source_target_pairs={{0,2},{2,4},{4,6},{6,8},{8,10},{10,12},{12,14},{14,16},{16,18},{18... | collective-permute-start | bytes 552968 | tf_op jit(solution)/shard_map/ppermute | solution.py:169
  127.3 10.7 %collective-permute-start.5 = (f32[1,90,512]{2,1,0:T(8,128)S(1)}, f32[1,90,512]{2,1,0:T(8,128)S(1)}, u32[]{:S(2)}, u32[]{:S(2)}) collective-permute-start(f32[1,90,512]{2,1,0:T(8,128)S(1)} %get-tuple-element.227), channel_id=1, source_target_pairs={{2,0},{4,2},{6,4},{8,6},{10,8},{12,10},{14,12},{16,14},{18,16},{20... | collective-permute-start | bytes 552968 | tf_op jit(solution)/shard_map/ppermute | solution.py:170
  138.7 3.4 collective-permute-start.6
  138.7 4.0 collective-permute-start.7
  190.1 12.1 %all-to-all-start.6 = ((f32[32,1,128]{2,1,0:T(1,128)}), f32[32,1,128]{2,1,0:T(1,128)}, u32[]{:S(2)}, u32[]{:S(2)}) async-start(f32[32,1,128]{2,1,0:T(1,128)} %broadcast_in_dim.53), calls=%async_computation.6 | async-start | bytes 32768 | tf_op jit(solution)/shard_map/all_to_all | solution.py:106
  208.8 11.2 %all-to-all-start.7 = ((f32[32,1,128]{2,1,0:T(1,128)}), f32[32,1,128]{2,1,0:T(1,128)}, u32[]{:S(2)}, u32[]{:S(2)}) async-start(f32[32,1,128]{2,1,0:T(1,128)} %broadcast_in_dim.54), calls=%async_computation.7 | async-start | bytes 32768 | tf_op jit(solution)/shard_map/all_to_all | solution.py:106
  222.2 31.0 %copy-start.14 = (f32[16,90,64]{1,2,0:T(8,128)}, f32[16,90,64]{1,2,0:T(8,128)S(1)}, u32[]{:S(2)}) copy-start(f32[16,90,64]{1,2,0:T(8,128)S(1)} %subtract_multiply_fusion.4) | copy-start | bytes 1105924
  240.2 8.1 %collective-permute-start.10 = (f32[1,90,64]{1,2,0:T(8,128)S(1)}, f32[1,90,64]{1,2,0:T(8,128)S(1)}, u32[]{:S(2)}, u32[]{:S(2)}) collective-permute-start(f32[1,90,64]{1,2,0:T(8,128)S(1)} %get-tuple-element.245), channel_id=1, source_target_pairs={{2,0},{4,2},{6,4},{8,6},{10,8},{12,10},{14,12},{16,14},{18,16},{20... | collective-permute-start | bytes 69128 | tf_op jit(solution)/shard_map/ppermute | solution.py:170
  245.7 7.5 %collective-permute-start.9 = (f32[1,90,64]{1,2,0:T(8,128)S(1)}, f32[1,90,64]{1,2,0:T(8,128)S(1)}, u32[]{:S(2)}, u32[]{:S(2)}) collective-permute-start(f32[1,90,64]{1,2,0:T(8,128)S(1)} %get-tuple-element.244), channel_id=1, source_target_pairs={{0,2},{2,4},{4,6},{6,8},{8,10},{10,12},{12,14},{14,16},{16,18},{18... | collective-permute-start | bytes 69128 | tf_op jit(solution)/shard_map/ppermute | solution.py:169
  256.4 10.5 %collective-permute-start.11 = (f32[18,1,64]{2,1,0:T(1,128)}, f32[18,1,64]{2,1,0:T(1,128)}, u32[]{:S(2)}, u32[]{:S(2)}) collective-permute-start(f32[18,1,64]{2,1,0:T(1,128)} %copy.139), channel_id=1, source_target_pairs={{0,1},{1,0},{2,3},{3,2},{4,5},{5,4},{6,7},{7,6},{8,9},{9,8},{10,11... | collective-permute-start | bytes 13832 | tf_op jit(solution)/shard_map/ppermute | solution.py:169
  258.3 9.6 %collective-permute-start.12 = (f32[18,1,64]{2,1,0:T(1,128)}, f32[18,1,64]{2,1,0:T(1,128)}, u32[]{:S(2)}, u32[]{:S(2)}) collective-permute-start(f32[18,1,64]{2,1,0:T(1,128)} %copy.140), channel_id=1, source_target_pairs={{1,0},{0,1},{3,2},{2,3},{5,4},{4,5},{7,6},{6,7},{9,8},{8,9},{11,10... | collective-permute-start | bytes 13832 | tf_op jit(solution)/shard_map/ppermute | solution.py:170
  308.0 10.0 %all-to-all-start.9 = ((f32[32,1,512]{2,1,0:T(1,128)}), f32[32,1,512]{2,1,0:T(1,128)S(1)}, u32[]{:S(2)}, u32[]{:S(2)}) async-start(f32[32,1,512]{2,1,0:T(1,128)} %broadcast_in_dim.56), calls=%async_computation.9 | async-start | bytes 131072 | tf_op jit(solution)/shard_map/all_to_all | solution.py:106
  315.7 105.8 %collective-permute-start.15 = (f32[16,144,64]{1,2,0:T(8,128)}, f32[16,144,64]{1,2,0:T(8,128)}, u32[]{:S(2)}, u32[]{:S(2)}) collective-permute-start(f32[16,144,64]{1,2,0:T(8,128)} %copy.186), channel_id=1, source_target_pairs={{0,1},{1,0},{2,3},{3,2},{4,5},{5,4},{6,7},{7,6},{8,9},{9,8},{10,11... | collective-permute-start | bytes 1769480 | tf_op jit(solution)/shard_map/ppermute | solution.py:100
  318.6 14.2 %all-to-all-start.8 = ((f32[32,1,512]{2,1,0:T(1,128)}), f32[32,1,512]{2,1,0:T(1,128)}, u32[]{:S(2)}, u32[]{:S(2)}) async-start(f32[32,1,512]{2,1,0:T(1,128)} %broadcast_in_dim.55), calls=%async_computation.8 | async-start | bytes 131072 | tf_op jit(solution)/shard_map/all_to_all | solution.py:106
  337.7 13.7 %collective-permute-start.23 = (f32[16,8,128]{2,1,0:T(8,128)}, f32[16,8,128]{2,1,0:T(8,128)}, u32[]{:S(2)}, u32[]{:S(2)}) collective-permute-start(f32[16,8,128]{2,1,0:T(8,128)} %constant_dynamic-slice_fusion), channel_id=1, source_target_pairs={{0,1},{1,0},{2,3},{3,2},{4,5},{5,4},{6,7},{7,6},{8,9},{9,8},{10,11... | collective-permute-start | bytes 196616 | tf_op jit(solution)/shard_map/ppermute | solution.py:100
  341.9 37.4 %collective-permute-start.20 = (f32[16,64,128]{2,1,0:T(8,128)}, f32[16,64,128]{2,1,0:T(8,128)}, u32[]{:S(2)}, u32[]{:S(2)}) collective-permute-start(f32[16,64,128]{2,1,0:T(8,128)} %constant_dynamic-slice_fusion.1), channel_id=1, source_target_pairs={{0,1},{1,0},{2,3},{3,2},{4,5},{5,4},{6,7},{7,6},{8,9},{9,8},{10,11... | collective-permute-start | bytes 1572872 | tf_op jit(solution)/shard_map/ppermute | solution.py:100
  345.7 13.2 %all-to-all-start.10 = ((f32[32,1,512]{2,1,0:T(1,128)}), f32[32,1,512]{2,1,0:T(1,128)S(1)}, u32[]{:S(2)}, u32[]{:S(2)}) async-start(f32[32,1,512]{2,1,0:T(1,128)} %broadcast_in_dim.57), calls=%async_computation.10 | async-start | bytes 131072 | tf_op jit(solution)/shard_map/all_to_all | solution.py:106
  358.8 12.9 %all-to-all-start.19 = ((f32[16,8,128]{2,1,0:T(8,128)}), f32[16,8,128]{2,1,0:T(8,128)S(1)}, u32[]{:S(2)}, u32[]{:S(2)}) async-start(f32[16,8,128]{2,1,0:T(8,128)} %dynamic-slice_add_fusion.2), calls=%async_computation.19 | async-start | bytes 131072 | tf_op jit(solution)/shard_map/all_to_all | solution.py:147
  370.3 28.4 %collective-permute-start.17 = (f32[16,72,128]{2,1,0:T(8,128)}, f32[16,72,128]{2,1,0:T(8,128)}, u32[]{:S(2)}, u32[]{:S(2)}) collective-permute-start(f32[16,72,128]{2,1,0:T(8,128)} %constant_dynamic-slice_fusion.2), channel_id=1, source_target_pairs={{0,1},{1,0},{2,3},{3,2},{4,5},{5,4},{6,7},{7,6},{8,9},{9,8},{10,11... | collective-permute-start | bytes 1769480 | tf_op jit(solution)/shard_map/ppermute | solution.py:100
  372.4 14.5 %all-to-all-start.20 = ((f32[16,8,128]{2,1,0:T(8,128)}), f32[16,8,128]{2,1,0:T(8,128)}, u32[]{:S(2)}, u32[]{:S(2)}) async-start(f32[16,8,128]{2,1,0:T(8,128)} %broadcast_in_dim.61), calls=%async_computation.20 | async-start | bytes 131072 | tf_op jit(solution)/shard_map/all_to_all | solution.py:106
  386.9 18.9 %all-to-all-start.16 = ((f32[16,64,128]{2,1,0:T(8,128)}), f32[16,64,128]{2,1,0:T(8,128)}, u32[]{:S(2)}, u32[]{:S(2)}) async-start(f32[16,64,128]{2,1,0:T(8,128)} %dynamic-slice_add_fusion.1), calls=%async_computation.16 | async-start | bytes 1048576 | tf_op jit(solution)/shard_map/all_to_all | solution.py:147
  392.4 18.9 %collective-permute-start.13 = (f32[8,1,256]{2,1,0:T(1,128)S(1)}, f32[8,1,256]{2,1,0:T(1,128)S(1)}, u32[]{:S(2)}, u32[]{:S(2)}) collective-permute-start(f32[8,1,256]{2,1,0:T(1,128)S(1)} %slice.502), channel_id=1, source_target_pairs={{1,0},{3,2},{5,4},{7,6},{9,8},{11,10},{13,12},{15,14},{17,16},{19,... | collective-permute-start | bytes 24584 | tf_op jit(solution)/shard_map/ppermute | solution.py:153
  405.8 19.6 %all-to-all-start.13 = ((f32[16,72,128]{2,1,0:T(8,128)}), f32[16,72,128]{2,1,0:T(8,128)}, u32[]{:S(2)}, u32[]{:S(2)}) async-start(f32[16,72,128]{2,1,0:T(8,128)} %dynamic-slice_add_fusion), calls=%async_computation.13 | async-start | bytes 1179648 | tf_op jit(solution)/shard_map/all_to_all | solution.py:147
  411.3 8.1 %collective-permute-start.14 = (f32[1,46,256]{2,1,0:T(8,128)S(1)}, f32[1,46,256]{2,1,0:T(8,128)S(1)}, u32[]{:S(2)}, u32[]{:S(2)}) collective-permute-start(f32[1,46,256]{2,1,0:T(8,128)S(1)} %pad_maximum_fusion.25), channel_id=1, source_target_pairs={{0,30},{2,0},{4,2},{6,4},{8,6},{10,8},{12,10},{14,12},{16,14},{18,... | collective-permute-start | bytes 141320 | tf_op jit(solution)/shard_map/ppermute | solution.py:159
  425.4 32.6 %all-to-all-start.11 = ((f32[16,144,64]{1,2,0:T(8,128)}), f32[16,144,64]{1,2,0:T(8,128)}, u32[]{:S(2)}, u32[]{:S(2)}) async-start(f32[16,144,64]{1,2,0:T(8,128)} %copy_add_fusion), calls=%async_computation.11 | async-start | bytes 2097152 | tf_op jit(solution)/shard_map/all_to_all | solution.py:147
  438.9 2.0 collective-permute-start.21
  439.0 36.7 %copy-start.23 = (f32[16,90,256]{2,1,0:T(8,128)S(1)}, f32[16,90,256]{2,1,0:T(8,128)}, u32[]{:S(2)}) copy-start(f32[16,90,256]{2,1,0:T(8,128)} %get-tuple-element.217) | copy-start | bytes 4423684
  439.0 36.7 %copy-start.66 = (f32[128,256]{1,0:T(8,128)S(1)}, f32[128,256]{1,0:T(8,128)}, u32[]{:S(2)}) copy-start(f32[128,256]{1,0:T(8,128)} %param.47) | copy-start | bytes 393220
  440.5 39.5 %collective-permute-start.24 = (f32[128,128]{1,0:T(8,128)}, f32[128,128]{1,0:T(8,128)}, u32[]{:S(2)}, u32[]{:S(2)}) collective-permute-start(f32[128,128]{1,0:T(8,128)} %bitcast.79), channel_id=1, source_target_pairs={{0,1},{1,0},{2,3},{3,2},{4,5},{5,4},{6,7},{7,6},{8,9},{9,8},{10,11... | collective-permute-start | bytes 196616 | tf_op jit(solution)/shard_map/ppermute | solution.py:100
  442.9 20.9 %collective-permute-start.18 = (f32[72,128]{1,0:T(8,128)S(1)}, f32[72,128]{1,0:T(8,128)}, u32[]{:S(2)}, u32[]{:S(2)}) collective-permute-start(f32[72,128]{1,0:T(8,128)S(1)} %reduce_sum.345), channel_id=1, source_target_pairs={{0,1},{1,0},{2,3},{3,2},{4,5},{5,4},{6,7},{7,6},{8,9},{9,8},{10,11... | collective-permute-start | bytes 110600 | tf_op jit(solution)/shard_map/ppermute | solution.py:100
  457.9 13.6 %all-to-all-start.17 = ((f32[16,16,128]{2,1,0:T(8,128)}), f32[16,16,128]{2,1,0:T(8,128)S(1)}, u32[]{:S(2)}, u32[]{:S(2)}) async-start(f32[16,16,128]{2,1,0:T(8,128)} %bitcast.314), calls=%async_computation.17 | async-start | bytes 262144 | tf_op jit(solution)/shard_map/all_to_all | solution.py:198
  472.2 11.3 %all-to-all-start.14 = ((f32[16,16,128]{2,1,0:T(8,128)}), f32[16,16,128]{2,1,0:T(8,128)S(1)}, u32[]{:S(2)}, u32[]{:S(2)}) async-start(f32[16,16,128]{2,1,0:T(8,128)} %bitcast.313), calls=%async_computation.14 | async-start | bytes 262144 | tf_op jit(solution)/shard_map/all_to_all | solution.py:198
  484.1 12.1 %all-to-all-start.18 = ((f32[16,16,128]{2,1,0:T(8,128)}), f32[16,16,128]{2,1,0:T(8,128)S(1)}, u32[]{:S(2)}, u32[]{:S(2)}) async-start(f32[16,16,128]{2,1,0:T(8,128)} %broadcast_in_dim.60), calls=%async_computation.18 | async-start | bytes 262144 | tf_op jit(solution)/shard_map/all_to_all | solution.py:106
  490.2 10.2 %collective-permute-start.16 = (f32[144,64]{0,1:T(8,128)S(1)}, f32[144,64]{0,1:T(8,128)S(1)}, u32[]{:S(2)}, u32[]{:S(2)}) collective-permute-start(f32[144,64]{0,1:T(8,128)S(1)} %reduce_sum.343), channel_id=1, source_target_pairs={{0,1},{1,0},{2,3},{3,2},{4,5},{5,4},{6,7},{7,6},{8,9},{9,8},{10,11... | collective-permute-start | bytes 110600 | tf_op jit(solution)/shard_map/ppermute | solution.py:100
  496.9 11.3 %all-to-all-start.15 = ((f32[16,16,128]{2,1,0:T(8,128)}), f32[16,16,128]{2,1,0:T(8,128)S(1)}, u32[]{:S(2)}, u32[]{:S(2)}) async-start(f32[16,16,128]{2,1,0:T(8,128)} %broadcast_in_dim.59), calls=%async_computation.15 | async-start | bytes 262144 | tf_op jit(solution)/shard_map/all_to_all | solution.py:106
  509.8 31.1 %all-to-all-start.12 = ((f32[32,1,8646]{2,1,0:T(1,128)}), f32[32,1,8646]{2,1,0:T(1,128)}, u32[]{:S(2)}, u32[]{:S(2)}) async-start(f32[32,1,8646]{2,1,0:T(1,128)} %broadcast_in_dim.58), calls=%async_computation.12 | async-start | bytes 2228224 | tf_op jit(solution)/shard_map/all_to_all | solution.py:106
  516.9 25.9 %copy-start.82 = (f32[72,256]{1,0:T(8,128)}, f32[72,256]{1,0:T(8,128)S(1)}, u32[]{:S(2)}) copy-start(f32[72,256]{1,0:T(8,128)S(1)} %get-tuple-element.258) | copy-start | bytes 221188
  516.9 25.9 %copy-start.83 = (f32[72,256]{1,0:T(8,128)}, f32[72,256]{1,0:T(8,128)S(1)}, u32[]{:S(2)}) copy-start(f32[72,256]{1,0:T(8,128)S(1)} %get-tuple-element.259) | copy-start | bytes 221188
  516.9 1.6 collective-permute-start.22
  518.1 1.4 collective-permute-start.19
  518.6 25.0 %copy-start.182 = (f32[64,70]{1,0:T(8,128)S(1)}, f32[64,70]{1,0:T(8,128)}, u32[]{:S(2)}) copy-start(f32[64,70]{1,0:T(8,128)} %param.57) | copy-start | bytes 53764
  518.6 25.8 %copy-start.116 = (f32[1734]{0:T(1024)S(1)}, f32[1734]{0:T(1024)}, u32[]{:S(2)}) copy-start(f32[1734]{0:T(1024)} %param.34) | copy-start | bytes 20812
  518.7 25.8 %copy-start.142 = (f32[1734]{0:T(1024)S(1)}, f32[1734]{0:T(1024)}, u32[]{:S(2)}) copy-start(f32[1734]{0:T(1024)} %param.35) | copy-start | bytes 20812
  518.7 25.8 %copy-start.143 = (f32[1734]{0:T(1024)S(1)}, f32[1734]{0:T(1024)}, u32[]{:S(2)}) copy-start(f32[1734]{0:T(1024)} %param.36) | copy-start | bytes 20812
  518.7 26.4 %copy-start.3 = (f32[256,256]{1,0:T(8,128)S(1)}, f32[256,256]{1,0:T(8,128)}, u32[]{:S(2)}) copy-start(f32[256,256]{1,0:T(8,128)} %refs_0_.1) | copy-start | bytes 786436
  518.7 26.4 %copy-start.4 = (f32[256,256]{1,0:T(8,128)S(1)}, f32[256,256]{1,0:T(8,128)}, u32[]{:S(2)}) copy-start(f32[256,256]{1,0:T(8,128)} %refs_1_.1) | copy-start | bytes 786436
  518.7 26.4 %copy-start.5 = (f32[256,256]{1,0:T(8,128)S(1)}, f32[256,256]{1,0:T(8,128)}, u32[]{:S(2)}) copy-start(f32[256,256]{1,0:T(8,128)} %refs_2_.1) | copy-start | bytes 786436
  518.7 26.4 %copy-start.8 = (f32[70,70]{1,0:T(8,128)S(1)}, f32[70,70]{1,0:T(8,128)}, u32[]{:S(2)}) copy-start(f32[70,70]{1,0:T(8,128)} %refs_4_.1) | copy-start | bytes 58804
  518.8 26.4 %copy-start.9 = (f32[64,64]{1,0:T(8,128)S(1)}, f32[64,64]{1,0:T(8,128)}, u32[]{:S(2)}) copy-start(f32[64,64]{1,0:T(8,128)} %refs_3_.1) | copy-start | bytes 49156
  543.6 38.6 %copy-start.113 = (f32[64,70]{1,0:T(8,128)}, f32[64,70]{1,0:T(8,128)S(1)}, u32[]{:S(2)}) copy-start(f32[64,70]{1,0:T(8,128)S(1)} %get-tuple-element.266) | copy-start | bytes 53764
  543.6 38.6 %copy-start.114 = (f32[64,70]{1,0:T(8,128)}, f32[64,70]{1,0:T(8,128)S(1)}, u32[]{:S(2)}) copy-start(f32[64,70]{1,0:T(8,128)S(1)} %get-tuple-element.267) | copy-start | bytes 53764
  (165 other events, 959.5 us)
